TPU v7x, 128 devices: a whole 4x4x4 slice. The times are simulated.
128 devices in a mesh: rows: 8 (over x_hi, z), cols: 16 (over x_lo, y, core).
Axes of the slice: x: 4 (x_hi: 2, x_lo: 2; x = x_hi * 2 + x_lo), y: 4, z: 4, core: 2. Of those that a mesh axis runs over, the one named last changes fastest.
Arguments:
- observed: float32 [426, 128, 2048], P(None, 'rows', 'cols'), may hold values from 0.05 to 3
- nonlin: float32 [128, 2048], P('rows', 'cols'), may hold values from -0.3 to 0.3
- abundance: float32 [64, 128, 2048], P(None, 'rows', 'cols'), may hold values from 0 to 2
- spectra: float32 [426, 64], replicated, may hold values from 0.1 to 1
- kernels: float32 [8, 9, 9], replicated, may hold values from 0.003 to 0.03
- tile_family: int32 [8, 16], P('rows', 'cols'), may hold values from 0 to 7
Outputs:
- abundance_out: float32 [64, 128, 2048], P(None, 'rows', 'cols')
- spectra_out: float32 [426, 64], replicated
All inputs are finite; a program needn't handle non-finite values.
Results may differ from a plain program's by a relative error of at most 0.0003.
Values sent between devices are 32-bit elements; how exact they have to be, the bound alone decides.
A program may use at most 64 MiB of HBM per device.

v0:
```python
import jax
import jax.numpy as jnp
from jax import lax
from jax.sharding import PartitionSpec as P

KS = 9
ITERS = 3


def padded_2(block, sides, width):
    for axis, dim in sides:
        count = lax.axis_size(axis)
        forward = [(i, i + 1) for i in range(count - 1)]
        backward = [(target, source) for source, target in forward]
        low = lax.ppermute(
            lax.slice_in_dim(block, block.shape[dim] - width, None, axis=dim), axis, forward
        )
        high = lax.ppermute(lax.slice_in_dim(block, 0, width, axis=dim), axis, backward)
        block = jnp.concatenate([low, block, high], axis=dim)
    return block


def shifted(block, axis, distance):
    devices = range(lax.axis_size(axis))
    route = [(i - distance, i) for i in devices if i - distance in devices]
    return lax.ppermute(block, axis, route)


def cut_along(x, dim, devices):
    before, after = (x.shape[:dim], x.shape[dim + 1 :])
    return jnp.moveaxis(x.reshape(*before, devices, -1, *after), dim, 0)


def sent_and_summed(x, axis, dim):
    devices = lax.axis_size(axis)
    blocks = lax.all_to_all(cut_along(x, dim, devices), axis, 0, 0, tiled=True)
    return jnp.sum(blocks, axis=0)


def from_everyone(x, axis):
    copies = jnp.broadcast_to(x, (lax.axis_size(axis), *x.shape))
    return lax.all_to_all(copies, axis, split_axis=0, concat_axis=0, tiled=True)


def of_everyone(x, axis):
    everything = from_everyone(x, axis)
    return jnp.sum(everything, axis=0)


def laid_out(blocks, dim):
    blocks = jnp.moveaxis(blocks, 0, dim)
    shape = blocks.shape
    return blocks.reshape(*shape[:dim], shape[dim] * shape[dim + 1], *shape[dim + 2 :])


def collect(x, axis, dim):
    return laid_out(from_everyone(x, axis), dim)


def offset_table(width, radius):
    padded_cols = jnp.arange(width + 2 * radius, dtype=jnp.int32)[:, None]
    out_cols = jnp.arange(width, dtype=jnp.int32)[None, :]
    offset = padded_cols - out_cols
    return (offset[None] == jnp.arange(KS, dtype=jnp.int32)[:, None, None]).astype(jnp.float32)


def on_device(observed, nonlin, abundance, spectra, kernels, tile_family):
    highest = lax.Precision.HIGHEST
    bands, height, width = observed.shape
    channels = abundance.shape[0]
    radius = KS // 2
    pixel_count = height * width * lax.axis_size("rows") * lax.axis_size("cols")
    table = kernels.reshape(kernels.shape[0], KS * KS)
    family_ids = jnp.arange(table.shape[0], dtype=jnp.int32)
    own_pick = (family_ids == tile_family[0, 0]).astype(jnp.float32)
    own_kernel = jnp.dot(
        own_pick, table, precision=highest, preferred_element_type=jnp.float32
    ).reshape(KS, KS)
    forward_bands = jnp.einsum(
        "uv,vpj->upj", own_kernel, offset_table(width, radius), precision=highest
    )
    flat_pixels = observed.reshape(bands, height * width)
    bend = nonlin.reshape(1, height * width)
    current = abundance
    endmembers = spectra
    for step in range(ITERS):
        padded = padded_2(current, (("rows", 1), ("cols", 2)), radius)
        blurred = jnp.zeros((channels, height, width), jnp.float32)
        for row_shift in range(KS):
            blurred = blurred + jnp.dot(
                padded[:, row_shift : row_shift + height, :],
                forward_bands[row_shift],
                precision=highest,
                preferred_element_type=jnp.float32,
            )
        flat_blur = blurred.reshape(channels, height * width)
        linear = (
            jnp.dot(endmembers, flat_blur, precision=highest, preferred_element_type=jnp.float32)
            / channels
        )
        resid = linear + bend * linear * linear - flat_pixels
        weighted = resid * (1.0 + 2.0 * bend * linear)
        grad_flat = (
            lax.dot_general(
                endmembers,
                weighted,
                (((0,), (0,)), ((), ())),
                precision=highest,
                preferred_element_type=jnp.float32,
            )
            / channels
        )
        grad_local = (
            lax.dot_general(
                weighted,
                flat_blur,
                (((1,), (1,)), ((), ())),
                precision=highest,
                preferred_element_type=jnp.float32,
            )
            / channels
        )
        grad_blur = grad_flat.reshape(channels, height, width)
        spread = jnp.zeros((channels, height + 2 * radius, width + 2 * radius), jnp.float32)
        for row_shift in range(KS):
            contrib = lax.dot_general(
                grad_blur,
                forward_bands[row_shift],
                (((2,), (1,)), ((), ())),
                precision=highest,
                preferred_element_type=jnp.float32,
            )
            spread = spread + jnp.pad(
                contrib, ((0, 0), (row_shift, 2 * radius - row_shift), (0, 0))
            )
        middle = spread[:, radius : radius + height, :]
        from_above = shifted(spread[:, radius + height :, :], "rows", 1)
        from_below = shifted(spread[:, :radius, :], "rows", -1)
        middle = middle.at[:, :radius, :].add(from_above)
        middle = middle.at[:, height - radius :, :].add(from_below)
        grad_abund = middle[:, :, radius : radius + width]
        from_left = shifted(middle[:, :, radius + width :], "cols", 1)
        from_right = shifted(middle[:, :, :radius], "cols", -1)
        grad_abund = grad_abund.at[:, :, :radius].add(from_left)
        grad_abund = grad_abund.at[:, :, width - radius :].add(from_right)
        share = sent_and_summed(grad_local, "cols", 1)
        share = of_everyone(share, "rows")
        share_width = share.shape[1]
        start = lax.axis_index("cols") * share_width
        own_spectra = lax.dynamic_slice_in_dim(endmembers, start, share_width, 1)
        updated = jnp.maximum(own_spectra - 40.0 * (share / pixel_count), 0.0)
        new_spectra = collect(updated, "cols", 1)
        current = jnp.maximum(current - 0.5 * grad_abund, 0.0)
        endmembers = new_spectra
    return (current, endmembers)


def solution(mesh):
    placed = (
        P(None, "rows", "cols"),
        P("rows", "cols"),
        P(None, "rows", "cols"),
        P(),
        P(),
        P("rows", "cols"),
    )
    return jax.shard_map(
        on_device,
        mesh=mesh,
        in_specs=placed,
        out_specs=(P(None, "rows", "cols"), P()),
        check_vma=False,
    )
```

profile of v0, /device:TPU:98, one launch (start us, length us, event | category | flops | bytes accessed | tf_op | source)
XLA Modules:
  0.0 343.2 jit_solution(4394553261313331666)
XLA Ops:
  1.8 2.7 collective-permute-start
  4.5 3.2 collective-permute-start.1
  10.5 4.4 %collective-permute-done.1 = f32[64,4,128]{2,1,0:T(4,128)S(1)} collective-permute-done((f32[64,4,128]{2,1,0:T(4,128)S(1)}, f32[64,4,128]{2,1,0:T(4,128)S(1)}, u32[]{:S(2)}, u32[]{:S(2)}) %collective-permute-start.1) | collective-permute-done | bytes 131104 | tf_op jit(solution)/shard_map/ppermute | solution.py:18
  16.0 3.8 %collective-permute-start.3 = (f32[64,24,4]{0,1,2:T(8,128)S(1)}, f32[64,24,4]{0,1,2:T(8,128)S(1)}, u32[]{:S(2)}, u32[]{:S(2)}) collective-permute-start(f32[64,24,4]{0,1,2:T(8,128)S(1)} %copy.10), channel_id=1, source_target_pairs={{1,0},{2,1},{3,2},{4,3},{5,4},{6,5},{7,6},{8,7},{9,8},{10,9},{11,1... | collective-permute-start | bytes 73736 | tf_op jit(solution)/shard_map/ppermute | solution.py:18
  19.8 2.1 collective-permute-start.2
  21.9 2.2 pad.165
  24.1 3.4 copy.25
  37.1 1.6 fusion.19
  39.1 3.8 %fusion.1 = f32[426,2048]{1,0:T(8,128)S(1)} fusion(f32[426,2048]{1,0:T(8,128)S(1)} %bitcast.210, f32[426,64]{0,1:T(8,128)S(1)} %copy-done.14, f32[2048]{0:T(1024)S(1)} %get-tuple-element.180, f32[2048]{0:T(1024)S(1)} %get-tuple-element.179, f32[8,8,16,128]{3,2,1,0:T(8,128)S(1)} %bitcast.257), kind=kOutput, calls=%fused_computation.4 | convolution fusion | flops 677019648 | bytes 7629312 | tf_op jit(solution)/shard_map/dot_general | solution.py:98
  42.9 2.6 fusion.6
  54.8 1.6 pad_add_fusion.2
  57.3 2.1 collective-permute-start.4
  59.4 3.4 %convolution_multiply_fusion.5 = f32[426,64]{0,1:T(8,128)S(1)} fusion(f32[426,2048]{1,0:T(8,128)S(1)} %fusion.1, f32[8,8,16,128]{3,2,1,0:T(8,128)S(1)} %bitcast.258), kind=kOutput, calls=%fused_computation.47 | convolution fusion | flops 670067328 | bytes 4123136 | tf_op jit(solution)/shard_map/dot_general | solution.py:114
  63.6 6.0 %all-to-all-start = ((f32[16,426,4]{1,2,0:T(4,128)}), f32[16,426,4]{1,2,0:T(4,128)}, u32[]{:S(2)}, u32[]{:S(2)}) async-start(f32[16,426,4]{1,2,0:T(4,128)} %bitcast.29), calls=%async_computation | async-start | bytes 262144 | tf_op jit(solution)/shard_map/all_to_all | solution.py:36
  69.7 3.1 collective-permute-start.5
  72.9 2.1 all-to-all-done
  76.6 5.1 %all-to-all-start.1 = ((f32[8,426,4]{1,2,0:T(4,128)}), f32[8,426,4]{1,2,0:T(4,128)}, u32[]{:S(2)}, u32[]{:S(2)}) async-start(f32[8,426,4]{1,2,0:T(4,128)} %broadcast_in_dim.22), calls=%async_computation.1 | async-start | bytes 131072 | tf_op jit(solution)/shard_map/all_to_all | solution.py:42
  86.0 1.9 collective-permute-start.6
  88.1 5.8 %collective-permute-start.7 = (f32[64,16,4]{2,1,0:T(8,128)}, f32[64,16,4]{2,1,0:T(8,128)}, u32[]{:S(2)}, u32[]{:S(2)}) collective-permute-start(f32[64,16,4]{2,1,0:T(8,128)} %get-tuple-element.165), channel_id=1, source_target_pairs={{1,0},{2,1},{3,2},{4,3},{5,4},{6,5},{7,6},{8,7},{9,8},{10,9},{11,1... | collective-permute-start | bytes 49160 | tf_op jit(solution)/shard_map/ppermute | solution.py:26
  94.8 3.8 %collective-permute-done.6 = f32[64,16,4]{2,1,0:T(8,128)S(1)} collective-permute-done((f32[64,16,4]{2,1,0:T(8,128)S(1)}, f32[64,16,4]{2,1,0:T(8,128)S(1)}, u32[]{:S(2)}, u32[]{:S(2)}) %collective-permute-start.6) | collective-permute-done | bytes 16416 | tf_op jit(solution)/shard_map/ppermute | solution.py:26
  98.8 2.1 scatter-add.44
  102.2 10.6 %scatter-add.45 = f32[64,16,128]{2,1,0:T(8,128)S(1)} dynamic-update-slice(f32[64,16,128]{2,1,0:T(8,128)S(1)} %scatter-add.44, f32[64,16,4]{2,1,0:T(8,128)S(1)} %slice_add_fusion.4, s32[]{:T(128)} %constant.303.clone.1, s32[]{:T(128)} %constant.303.clone.1, s32[]{:T(128)} %constant.305.clone.1) | dynamic-update-slice | bytes 32772 | tf_op jit(solution)/shard_map/scatter-add | solution.py:145
  112.9 3.7 %collective-permute-start.8 = (f32[64,4,128]{2,1,0:T(4,128)S(1)}, f32[64,4,128]{2,1,0:T(4,128)S(1)}, u32[]{:S(2)}, u32[]{:S(2)}) collective-permute-start(f32[64,4,128]{2,1,0:T(4,128)S(1)} %get-tuple-element.175), channel_id=1, source_target_pairs={{0,16},{16,32},{32,48},{48,64},{64,80},{80,96},{96,112},{1,17},{17... | collective-permute-start | bytes 393224 | tf_op jit(solution)/shard_map/ppermute | solution.py:15
  116.6 2.2 collective-permute-start.9
  120.2 5.9 %all-to-all-start.2 = ((f32[16,426,4]{1,2,0:T(4,128)}), f32[16,426,4]{1,2,0:T(4,128)S(1)}, u32[]{:S(2)}, u32[]{:S(2)}) async-start(f32[16,426,4]{1,2,0:T(4,128)} %broadcast_in_dim.23), calls=%async_computation.2 | async-start | bytes 262144 | tf_op jit(solution)/shard_map/all_to_all | solution.py:42
  127.8 1.9 collective-permute-start.10
  130.0 6.2 %collective-permute-start.11 = (f32[64,24,4]{0,1,2:T(8,128)S(1)}, f32[64,24,4]{0,1,2:T(8,128)S(1)}, u32[]{:S(2)}, u32[]{:S(2)}) collective-permute-start(f32[64,24,4]{0,1,2:T(8,128)S(1)} %copy.15), channel_id=1, source_target_pairs={{1,0},{2,1},{3,2},{4,3},{5,4},{6,5},{7,6},{8,7},{9,8},{10,9},{11,1... | collective-permute-start | bytes 73736 | tf_op jit(solution)/shard_map/ppermute | solution.py:18
  148.8 3.9 %fusion.3 = f32[426,2048]{1,0:T(8,128)S(1)} fusion(f32[426,2048]{1,0:T(8,128)S(1)} %bitcast.211, f32[426,64]{0,1:T(8,128)S(1)} %reshape.419, f32[2048]{0:T(1024)S(1)} %get-tuple-element.180, f32[2048]{0:T(1024)S(1)} %get-tuple-element.179, f32[8,8,16,128]{3,2,1,0:T(8,128)S(1)} %bitcast.259), kind=kOutput, calls=%fused_computation.6 | convolution fusion | flops 677019648 | bytes 7629312 | tf_op jit(solution)/shard_map/dot_general | solution.py:98
  152.7 2.2 fusion.7
  164.2 1.6 pad_add_fusion.1
  167.8 5.7 %collective-permute-start.12 = (f32[64,4,136]{2,1,0:T(4,128)}, f32[64,4,136]{2,1,0:T(4,128)S(1)}, u32[]{:S(2)}, u32[]{:S(2)}) collective-permute-start(f32[64,4,136]{2,1,0:T(4,128)} %get-tuple-element.149), channel_id=1, source_target_pairs={{0,16},{16,32},{32,48},{48,64},{64,80},{80,96},{96,112},{1,17},{17... | collective-permute-start | bytes 417800 | tf_op jit(solution)/shard_map/ppermute | solution.py:26
  173.5 3.4 %convolution_multiply_fusion.4 = f32[426,64]{0,1:T(8,128)S(1)} fusion(f32[426,2048]{1,0:T(8,128)S(1)} %fusion.3, f32[8,8,16,128]{3,2,1,0:T(8,128)S(1)} %bitcast.260), kind=kOutput, calls=%fused_computation.46 | convolution fusion | flops 670067328 | bytes 4123136 | tf_op jit(solution)/shard_map/dot_general | solution.py:114
  177.6 6.1 %all-to-all-start.3 = ((f32[16,426,4]{1,2,0:T(4,128)}), f32[16,426,4]{1,2,0:T(4,128)S(1)}, u32[]{:S(2)}, u32[]{:S(2)}) async-start(f32[16,426,4]{1,2,0:T(4,128)} %bitcast.31), calls=%async_computation.3 | async-start | bytes 262144 | tf_op jit(solution)/shard_map/all_to_all | solution.py:36
  185.2 1.9 collective-permute-start.13
  187.2 1.8 all-to-all-done.3
  189.6 5.7 %all-to-all-start.4 = ((f32[8,426,4]{1,2,0:T(4,128)}), f32[8,426,4]{1,2,0:T(4,128)S(1)}, u32[]{:S(2)}, u32[]{:S(2)}) async-start(f32[8,426,4]{1,2,0:T(4,128)} %broadcast_in_dim.24), calls=%async_computation.4 | async-start | bytes 131072 | tf_op jit(solution)/shard_map/all_to_all | solution.py:42
  196.5 3.1 collective-permute-done.13
  200.6 1.9 collective-permute-start.14
  202.7 5.8 %collective-permute-start.15 = (f32[64,16,4]{2,1,0:T(8,128)}, f32[64,16,4]{2,1,0:T(8,128)}, u32[]{:S(2)}, u32[]{:S(2)}) collective-permute-start(f32[64,16,4]{2,1,0:T(8,128)} %get-tuple-element.163), channel_id=1, source_target_pairs={{1,0},{2,1},{3,2},{4,3},{5,4},{6,5},{7,6},{8,7},{9,8},{10,9},{11,1... | collective-permute-start | bytes 49160 | tf_op jit(solution)/shard_map/ppermute | solution.py:26
  208.5 4.8 %collective-permute-done.14 = f32[64,16,4]{2,1,0:T(8,128)} collective-permute-done((f32[64,16,4]{2,1,0:T(8,128)S(1)}, f32[64,16,4]{2,1,0:T(8,128)}, u32[]{:S(2)}, u32[]{:S(2)}) %collective-permute-start.14) | collective-permute-done | bytes 16416 | tf_op jit(solution)/shard_map/ppermute | solution.py:26
  214.6 2.1 scatter-add.50
  217.9 10.6 %scatter-add.51 = f32[64,16,128]{2,1,0:T(8,128)S(1)} dynamic-update-slice(f32[64,16,128]{2,1,0:T(8,128)S(1)} %scatter-add.50, f32[64,16,4]{2,1,0:T(8,128)S(1)} %slice_add_fusion.2, s32[]{:T(128)} %constant.303.clone.1, s32[]{:T(128)} %constant.303.clone.1, s32[]{:T(128)} %constant.305.clone.1) | dynamic-update-slice | bytes 32772 | tf_op jit(solution)/shard_map/scatter-add | solution.py:145
  228.7 1.9 collective-permute-start.16
  230.6 3.9 %collective-permute-start.17 = (f32[64,4,128]{2,1,0:T(4,128)S(1)}, f32[64,4,128]{2,1,0:T(4,128)S(1)}, u32[]{:S(2)}, u32[]{:S(2)}) collective-permute-start(f32[64,4,128]{2,1,0:T(4,128)S(1)} %get-tuple-element.174), channel_id=1, source_target_pairs={{16,0},{32,16},{48,32},{64,48},{80,64},{96,80},{112,96},{17,1},{33... | collective-permute-start | bytes 393224 | tf_op jit(solution)/shard_map/ppermute | solution.py:18
  235.2 4.1 %all-to-all-start.5 = ((f32[16,426,4]{1,2,0:T(4,128)}), f32[16,426,4]{1,2,0:T(4,128)S(1)}, u32[]{:S(2)}, u32[]{:S(2)}) async-start(f32[16,426,4]{1,2,0:T(4,128)} %broadcast_in_dim.25), calls=%async_computation.5 | async-start | bytes 262144 | tf_op jit(solution)/shard_map/all_to_all | solution.py:42
  239.4 1.7 collective-permute-done.17
  241.8 1.9 collective-permute-start.18
  244.0 6.2 %collective-permute-start.19 = (f32[64,24,4]{0,1,2:T(8,128)S(1)}, f32[64,24,4]{0,1,2:T(8,128)S(1)}, u32[]{:S(2)}, u32[]{:S(2)}) collective-permute-start(f32[64,24,4]{0,1,2:T(8,128)S(1)} %copy.19), channel_id=1, source_target_pairs={{1,0},{2,1},{3,2},{4,3},{5,4},{6,5},{7,6},{8,7},{9,8},{10,9},{11,1... | collective-permute-start | bytes 73736 | tf_op jit(solution)/shard_map/ppermute | solution.py:18
  262.7 3.9 %fusion.5 = f32[426,2048]{1,0:T(8,128)S(1)} fusion(f32[426,2048]{1,0:T(8,128)S(1)} %bitcast.212, f32[426,64]{0,1:T(8,128)S(1)} %reshape.423, f32[2048]{0:T(1024)S(1)} %get-tuple-element.180, f32[2048]{0:T(1024)S(1)} %get-tuple-element.179, f32[8,8,16,128]{3,2,1,0:T(8,128)S(1)} %bitcast.255), kind=kOutput, calls=%fused_computation.8 | convolution fusion | flops 677019648 | bytes 7629312 | tf_op jit(solution)/shard_map/dot_general | solution.py:98
  266.6 2.2 fusion.8
  278.1 1.6 pad_add_fusion
  280.6 3.7 %collective-permute-start.20 = (f32[64,4,136]{2,1,0:T(4,128)}, f32[64,4,136]{2,1,0:T(4,128)S(1)}, u32[]{:S(2)}, u32[]{:S(2)}) collective-permute-start(f32[64,4,136]{2,1,0:T(4,128)} %get-tuple-element.147), channel_id=1, source_target_pairs={{0,16},{16,32},{32,48},{48,64},{64,80},{80,96},{96,112},{1,17},{17... | collective-permute-start | bytes 417800 | tf_op jit(solution)/shard_map/ppermute | solution.py:26
  284.3 3.4 %convolution_multiply_fusion.3 = f32[426,64]{0,1:T(8,128)S(1)} fusion(f32[426,2048]{1,0:T(8,128)S(1)} %fusion.5, f32[8,8,16,128]{3,2,1,0:T(8,128)S(1)} %bitcast.256), kind=kOutput, calls=%fused_computation.45 | convolution fusion | flops 670067328 | bytes 4123136 | tf_op jit(solution)/shard_map/dot_general | solution.py:114
  288.5 6.0 %all-to-all-start.6 = ((f32[16,426,4]{1,2,0:T(4,128)}), f32[16,426,4]{1,2,0:T(4,128)S(1)}, u32[]{:S(2)}, u32[]{:S(2)}) async-start(f32[16,426,4]{1,2,0:T(4,128)} %bitcast.33), calls=%async_computation.6 | async-start | bytes 262144 | tf_op jit(solution)/shard_map/all_to_all | solution.py:36
  294.7 1.9 collective-permute-start.21
  296.6 3.2 all-to-all-done.6
  300.5 4.5 %all-to-all-start.7 = ((f32[8,426,4]{1,2,0:T(4,128)}), f32[8,426,4]{1,2,0:T(4,128)S(1)}, u32[]{:S(2)}, u32[]{:S(2)}) async-start(f32[8,426,4]{1,2,0:T(4,128)} %broadcast_in_dim.26), calls=%async_computation.7 | async-start | bytes 131072 | tf_op jit(solution)/shard_map/all_to_all | solution.py:42
  305.1 4.0 %collective-permute-done.21 = f32[64,4,136]{2,1,0:T(4,128)} collective-permute-done((f32[64,4,136]{2,1,0:T(4,128)}, f32[64,4,136]{2,1,0:T(4,128)}, u32[]{:S(2)}, u32[]{:S(2)}) %collective-permute-start.21) | collective-permute-done | bytes 139296 | tf_op jit(solution)/shard_map/ppermute | solution.py:26
  311.4 3.1 collective-permute-start.23
  314.5 1.9 collective-permute-start.22
  317.9 5.7 %all-to-all-start.8 = ((f32[16,426,4]{1,2,0:T(4,128)}), f32[16,426,4]{1,2,0:T(4,128)S(1)}, u32[]{:S(2)}, u32[]{:S(2)}) async-start(f32[16,426,4]{1,2,0:T(4,128)} %broadcast_in_dim.27), calls=%async_computation.8 | async-start | bytes 262144 | tf_op jit(solution)/shard_map/all_to_all | solution.py:42
  323.6 3.6 %collective-permute-done.22 = f32[64,16,4]{2,1,0:T(8,128)} collective-permute-done((f32[64,16,4]{2,1,0:T(8,128)S(1)}, f32[64,16,4]{2,1,0:T(8,128)}, u32[]{:S(2)}, u32[]{:S(2)}) %collective-permute-start.22) | collective-permute-done | bytes 16416 | tf_op jit(solution)/shard_map/ppermute | solution.py:26
  328.5 2.1 scatter-add.56
  330.8 10.6 %scatter-add.59 = f32[64,16,128]{2,1,0:T(8,128)S(1)} dynamic-update-slice(f32[64,16,128]{2,1,0:T(8,128)S(1)} %scatter-add.56, f32[64,16,4]{2,1,0:T(8,128)S(1)} %slice_add_fusion, s32[]{:T(128)} %constant.303.clone.1, s32[]{:T(128)} %constant.303.clone.1, s32[]{:T(128)} %constant.305.clone.1) | dynamic-update-slice | bytes 32772 | tf_op jit(solution)/shard_map/scatter-add | solution.py:145
  (191 shorter events, 101.0 us)
Async XLA Ops:
  0.6 14.3 %copy-start.1 = (f32[64,16,128]{2,1,0:T(8,128)S(1)}, f32[64,16,128]{2,1,0:T(8,128)}, u32[]{:S(2)}) copy-start(f32[64,16,128]{2,1,0:T(8,128)} %param.32) | copy-start | bytes 1572868
  1.8 8.7 %collective-permute-start = (f32[64,4,128]{2,1,0:T(4,128)S(1)}, f32[64,4,128]{2,1,0:T(4,128)S(1)}, u32[]{:S(2)}, u32[]{:S(2)}) collective-permute-start(f32[64,4,128]{2,1,0:T(4,128)S(1)} %get-tuple-element.177), channel_id=1, source_target_pairs={{0,16},{16,32},{32,48},{48,64},{64,80},{80,96},{96,112},{1,17},{17... | collective-permute-start | bytes 393224 | tf_op jit(solution)/shard_map/ppermute | solution.py:15
  4.5 10.5 %collective-permute-start.1 = (f32[64,4,128]{2,1,0:T(4,128)S(1)}, f32[64,4,128]{2,1,0:T(4,128)S(1)}, u32[]{:S(2)}, u32[]{:S(2)}) collective-permute-start(f32[64,4,128]{2,1,0:T(4,128)S(1)} %get-tuple-element.178), channel_id=1, source_target_pairs={{16,0},{32,16},{48,32},{64,48},{80,64},{96,80},{112,96},{17,1},{33... | collective-permute-start | bytes 393224 | tf_op jit(solution)/shard_map/ppermute | solution.py:18
  10.4 35.2 %copy-start.7 = (f32[1,136,128]{2,0,1:T(1,128)}, f32[1,136,128]{2,0,1:T(1,128)S(1)}, u32[]{:S(2)}) copy-start(f32[1,136,128]{2,0,1:T(1,128)S(1)} %get-tuple-element.153) | copy-start | bytes 208900
  10.5 36.2 %copy-start.11 = (f32[1,136,128]{2,0,1:T(1,128)}, f32[1,136,128]{2,0,1:T(1,128)S(1)}, u32[]{:S(2)}) copy-start(f32[1,136,128]{2,0,1:T(1,128)S(1)} %get-tuple-element.154) | copy-start | bytes 208900
  10.5 37.2 %copy-start.9 = (f32[1,136,128]{2,0,1:T(1,128)}, f32[1,136,128]{2,0,1:T(1,128)S(1)}, u32[]{:S(2)}) copy-start(f32[1,136,128]{2,0,1:T(1,128)S(1)} %get-tuple-element.155) | copy-start | bytes 208900
  10.5 38.2 %copy-start.5 = (f32[1,136,128]{2,0,1:T(1,128)}, f32[1,136,128]{2,0,1:T(1,128)S(1)}, u32[]{:S(2)}) copy-start(f32[1,136,128]{2,0,1:T(1,128)S(1)} %get-tuple-element.156) | copy-start | bytes 208900
  15.3 6.6 %copy-start.15 = (f32[16,128]{1,0:T(8,128)S(1)}, f32[16,128]{1,0:T(8,128)}, u32[]{:S(2)}) copy-start(f32[16,128]{1,0:T(8,128)} %param.31) | copy-start | bytes 24580
  16.0 11.9 %collective-permute-start.3 = (f32[64,24,4]{0,1,2:T(8,128)S(1)}, f32[64,24,4]{0,1,2:T(8,128)S(1)}, u32[]{:S(2)}, u32[]{:S(2)}) collective-permute-start(f32[64,24,4]{0,1,2:T(8,128)S(1)} %copy.10), channel_id=1, source_target_pairs={{1,0},{2,1},{3,2},{4,3},{5,4},{6,5},{7,6},{8,7},{9,8},{10,9},{11,1... | collective-permute-start | bytes 73736 | tf_op jit(solution)/shard_map/ppermute | solution.py:18
  19.8 7.7 %collective-permute-start.2 = (f32[64,24,4]{0,1,2:T(8,128)S(1)}, f32[64,24,4]{0,1,2:T(8,128)S(1)}, u32[]{:S(2)}, u32[]{:S(2)}) collective-permute-start(f32[64,24,4]{0,1,2:T(8,128)S(1)} %copy.9), channel_id=1, source_target_pairs={{0,1},{1,2},{2,3},{3,4},{4,5},{5,6},{6,7},{7,8},{8,9},{9,10},{10,1... | collective-permute-start | bytes 73736 | tf_op jit(solution)/shard_map/ppermute | solution.py:15
  37.1 2.0 copy-start.2
  37.1 2.0 copy-start.14
  57.3 24.4 %collective-permute-start.4 = (f32[64,4,136]{2,1,0:T(4,128)}, f32[64,4,136]{2,1,0:T(4,128)}, u32[]{:S(2)}, u32[]{:S(2)}) collective-permute-start(f32[64,4,136]{2,1,0:T(4,128)} %get-tuple-element.151), channel_id=1, source_target_pairs={{0,16},{16,32},{32,48},{48,64},{64,80},{80,96},{96,112},{1,17},{17... | collective-permute-start | bytes 417800 | tf_op jit(solution)/shard_map/ppermute | solution.py:26
  63.6 11.4 %all-to-all-start = ((f32[16,426,4]{1,2,0:T(4,128)}), f32[16,426,4]{1,2,0:T(4,128)}, u32[]{:S(2)}, u32[]{:S(2)}) async-start(f32[16,426,4]{1,2,0:T(4,128)} %bitcast.29), calls=%async_computation | async-start | bytes 262144 | tf_op jit(solution)/shard_map/all_to_all | solution.py:36
  69.7 14.3 %collective-permute-start.5 = (f32[64,4,136]{2,1,0:T(4,128)}, f32[64,4,136]{2,1,0:T(4,128)}, u32[]{:S(2)}, u32[]{:S(2)}) collective-permute-start(f32[64,4,136]{2,1,0:T(4,128)} %get-tuple-element.150), channel_id=1, source_target_pairs={{16,0},{32,16},{48,32},{64,48},{80,64},{96,80},{112,96},{17,1},{33... | collective-permute-start | bytes 417800 | tf_op jit(solution)/shard_map/ppermute | solution.py:26
  76.6 17.3 %all-to-all-start.1 = ((f32[8,426,4]{1,2,0:T(4,128)}), f32[8,426,4]{1,2,0:T(4,128)}, u32[]{:S(2)}, u32[]{:S(2)}) async-start(f32[8,426,4]{1,2,0:T(4,128)} %broadcast_in_dim.22), calls=%async_computation.1 | async-start | bytes 131072 | tf_op jit(solution)/shard_map/all_to_all | solution.py:42
  86.0 12.6 %collective-permute-start.6 = (f32[64,16,4]{2,1,0:T(8,128)S(1)}, f32[64,16,4]{2,1,0:T(8,128)S(1)}, u32[]{:S(2)}, u32[]{:S(2)}) collective-permute-start(f32[64,16,4]{2,1,0:T(8,128)S(1)} %get-tuple-element.166), channel_id=1, source_target_pairs={{0,1},{1,2},{2,3},{3,4},{4,5},{5,6},{6,7},{7,8},{8,9},{9,10},{10,1... | collective-permute-start | bytes 49160 | tf_op jit(solution)/shard_map/ppermute | solution.py:26
  88.1 12.8 %collective-permute-start.7 = (f32[64,16,4]{2,1,0:T(8,128)}, f32[64,16,4]{2,1,0:T(8,128)}, u32[]{:S(2)}, u32[]{:S(2)}) collective-permute-start(f32[64,16,4]{2,1,0:T(8,128)} %get-tuple-element.165), channel_id=1, source_target_pairs={{1,0},{2,1},{3,2},{4,3},{5,4},{6,5},{7,6},{8,7},{9,8},{10,9},{11,1... | collective-permute-start | bytes 49160 | tf_op jit(solution)/shard_map/ppermute | solution.py:26
  112.9 13.2 %collective-permute-start.8 = (f32[64,4,128]{2,1,0:T(4,128)S(1)}, f32[64,4,128]{2,1,0:T(4,128)S(1)}, u32[]{:S(2)}, u32[]{:S(2)}) collective-permute-start(f32[64,4,128]{2,1,0:T(4,128)S(1)} %get-tuple-element.175), channel_id=1, source_target_pairs={{0,16},{16,32},{32,48},{48,64},{64,80},{80,96},{96,112},{1,17},{17... | collective-permute-start | bytes 393224 | tf_op jit(solution)/shard_map/ppermute | solution.py:15
  116.6 10.5 %collective-permute-start.9 = (f32[64,4,128]{2,1,0:T(4,128)S(1)}, f32[64,4,128]{2,1,0:T(4,128)S(1)}, u32[]{:S(2)}, u32[]{:S(2)}) collective-permute-start(f32[64,4,128]{2,1,0:T(4,128)S(1)} %get-tuple-element.176), channel_id=1, source_target_pairs={{16,0},{32,16},{48,32},{64,48},{80,64},{96,80},{112,96},{17,1},{33... | collective-permute-start | bytes 393224 | tf_op jit(solution)/shard_map/ppermute | solution.py:18
  120.2 16.0 %all-to-all-start.2 = ((f32[16,426,4]{1,2,0:T(4,128)}), f32[16,426,4]{1,2,0:T(4,128)S(1)}, u32[]{:S(2)}, u32[]{:S(2)}) async-start(f32[16,426,4]{1,2,0:T(4,128)} %broadcast_in_dim.23), calls=%async_computation.2 | async-start | bytes 262144 | tf_op jit(solution)/shard_map/all_to_all | solution.py:42
  127.8 8.5 %collective-permute-start.10 = (f32[64,24,4]{0,1,2:T(8,128)S(1)}, f32[64,24,4]{0,1,2:T(8,128)S(1)}, u32[]{:S(2)}, u32[]{:S(2)}) collective-permute-start(f32[64,24,4]{0,1,2:T(8,128)S(1)} %copy.14), channel_id=1, source_target_pairs={{0,1},{1,2},{2,3},{3,4},{4,5},{5,6},{6,7},{7,8},{8,9},{9,10},{10,1... | collective-permute-start | bytes 73736 | tf_op jit(solution)/shard_map/ppermute | solution.py:15
  130.0 7.5 %collective-permute-start.11 = (f32[64,24,4]{0,1,2:T(8,128)S(1)}, f32[64,24,4]{0,1,2:T(8,128)S(1)}, u32[]{:S(2)}, u32[]{:S(2)}) collective-permute-start(f32[64,24,4]{0,1,2:T(8,128)S(1)} %copy.15), channel_id=1, source_target_pairs={{1,0},{2,1},{3,2},{4,3},{5,4},{6,5},{7,6},{8,7},{9,8},{10,9},{11,1... | collective-permute-start | bytes 73736 | tf_op jit(solution)/shard_map/ppermute | solution.py:18
  137.9 1.0 copy-start.8
  138.9 1.0 copy-start.12
  138.9 2.0 copy-start.10
  139.9 2.0 copy-start.6
  146.8 2.0 copy-start.3
  165.8 1.2 copy-start
  167.8 27.6 %collective-permute-start.12 = (f32[64,4,136]{2,1,0:T(4,128)}, f32[64,4,136]{2,1,0:T(4,128)S(1)}, u32[]{:S(2)}, u32[]{:S(2)}) collective-permute-start(f32[64,4,136]{2,1,0:T(4,128)} %get-tuple-element.149), channel_id=1, source_target_pairs={{0,16},{16,32},{32,48},{48,64},{64,80},{80,96},{96,112},{1,17},{17... | collective-permute-start | bytes 417800 | tf_op jit(solution)/shard_map/ppermute | solution.py:26
  177.6 11.4 %all-to-all-start.3 = ((f32[16,426,4]{1,2,0:T(4,128)}), f32[16,426,4]{1,2,0:T(4,128)S(1)}, u32[]{:S(2)}, u32[]{:S(2)}) async-start(f32[16,426,4]{1,2,0:T(4,128)} %bitcast.31), calls=%async_computation.3 | async-start | bytes 262144 | tf_op jit(solution)/shard_map/all_to_all | solution.py:36
  185.2 14.3 %collective-permute-start.13 = (f32[64,4,136]{2,1,0:T(4,128)S(1)}, f32[64,4,136]{2,1,0:T(4,128)S(1)}, u32[]{:S(2)}, u32[]{:S(2)}) collective-permute-start(f32[64,4,136]{2,1,0:T(4,128)S(1)} %get-tuple-element.148), channel_id=1, source_target_pairs={{16,0},{32,16},{48,32},{64,48},{80,64},{96,80},{112,96},{17,1},{33... | collective-permute-start | bytes 417800 | tf_op jit(solution)/shard_map/ppermute | solution.py:26
  189.6 18.9 %all-to-all-start.4 = ((f32[8,426,4]{1,2,0:T(4,128)}), f32[8,426,4]{1,2,0:T(4,128)S(1)}, u32[]{:S(2)}, u32[]{:S(2)}) async-start(f32[8,426,4]{1,2,0:T(4,128)} %broadcast_in_dim.24), calls=%async_computation.4 | async-start | bytes 131072 | tf_op jit(solution)/shard_map/all_to_all | solution.py:42
  200.6 12.7 %collective-permute-start.14 = (f32[64,16,4]{2,1,0:T(8,128)S(1)}, f32[64,16,4]{2,1,0:T(8,128)}, u32[]{:S(2)}, u32[]{:S(2)}) collective-permute-start(f32[64,16,4]{2,1,0:T(8,128)S(1)} %get-tuple-element.164), channel_id=1, source_target_pairs={{0,1},{1,2},{2,3},{3,4},{4,5},{5,6},{6,7},{7,8},{8,9},{9,10},{10,1... | collective-permute-start | bytes 49160 | tf_op jit(solution)/shard_map/ppermute | solution.py:26
  202.7 13.9 %collective-permute-start.15 = (f32[64,16,4]{2,1,0:T(8,128)}, f32[64,16,4]{2,1,0:T(8,128)}, u32[]{:S(2)}, u32[]{:S(2)}) collective-permute-start(f32[64,16,4]{2,1,0:T(8,128)} %get-tuple-element.163), channel_id=1, source_target_pairs={{1,0},{2,1},{3,2},{4,3},{5,4},{6,5},{7,6},{8,7},{9,8},{10,9},{11,1... | collective-permute-start | bytes 49160 | tf_op jit(solution)/shard_map/ppermute | solution.py:26
  228.7 10.7 %collective-permute-start.16 = (f32[64,4,128]{2,1,0:T(4,128)S(1)}, f32[64,4,128]{2,1,0:T(4,128)S(1)}, u32[]{:S(2)}, u32[]{:S(2)}) collective-permute-start(f32[64,4,128]{2,1,0:T(4,128)S(1)} %get-tuple-element.173), channel_id=1, source_target_pairs={{0,16},{16,32},{32,48},{48,64},{64,80},{80,96},{96,112},{1,17},{17... | collective-permute-start | bytes 393224 | tf_op jit(solution)/shard_map/ppermute | solution.py:15
  230.6 10.5 %collective-permute-start.17 = (f32[64,4,128]{2,1,0:T(4,128)S(1)}, f32[64,4,128]{2,1,0:T(4,128)S(1)}, u32[]{:S(2)}, u32[]{:S(2)}) collective-permute-start(f32[64,4,128]{2,1,0:T(4,128)S(1)} %get-tuple-element.174), channel_id=1, source_target_pairs={{16,0},{32,16},{48,32},{64,48},{80,64},{96,80},{112,96},{17,1},{33... | collective-permute-start | bytes 393224 | tf_op jit(solution)/shard_map/ppermute | solution.py:18
  235.2 15.0 %all-to-all-start.5 = ((f32[16,426,4]{1,2,0:T(4,128)}), f32[16,426,4]{1,2,0:T(4,128)S(1)}, u32[]{:S(2)}, u32[]{:S(2)}) async-start(f32[16,426,4]{1,2,0:T(4,128)} %broadcast_in_dim.25), calls=%async_computation.5 | async-start | bytes 262144 | tf_op jit(solution)/shard_map/all_to_all | solution.py:42
  241.8 8.5 %collective-permute-start.18 = (f32[64,24,4]{0,1,2:T(8,128)S(1)}, f32[64,24,4]{0,1,2:T(8,128)S(1)}, u32[]{:S(2)}, u32[]{:S(2)}) collective-permute-start(f32[64,24,4]{0,1,2:T(8,128)S(1)} %copy.18), channel_id=1, source_target_pairs={{0,1},{1,2},{2,3},{3,4},{4,5},{5,6},{6,7},{7,8},{8,9},{9,10},{10,1... | collective-permute-start | bytes 73736 | tf_op jit(solution)/shard_map/ppermute | solution.py:15
  244.0 7.5 %collective-permute-start.19 = (f32[64,24,4]{0,1,2:T(8,128)S(1)}, f32[64,24,4]{0,1,2:T(8,128)S(1)}, u32[]{:S(2)}, u32[]{:S(2)}) collective-permute-start(f32[64,24,4]{0,1,2:T(8,128)S(1)} %copy.19), channel_id=1, source_target_pairs={{1,0},{2,1},{3,2},{4,3},{5,4},{6,5},{7,6},{8,7},{9,8},{10,9},{11,1... | collective-permute-start | bytes 73736 | tf_op jit(solution)/shard_map/ppermute | solution.py:18
  250.2 16.3 %copy-start.13 = (f32[426,64]{0,1:T(8,128)}, f32[426,64]{0,1:T(8,128)S(1)}, u32[]{:S(2)}) copy-start(f32[426,64]{0,1:T(8,128)S(1)} %reshape.423) | copy-start | bytes 327172
  260.7 2.0 copy-start.4
  280.6 24.4 %collective-permute-start.20 = (f32[64,4,136]{2,1,0:T(4,128)}, f32[64,4,136]{2,1,0:T(4,128)S(1)}, u32[]{:S(2)}, u32[]{:S(2)}) collective-permute-start(f32[64,4,136]{2,1,0:T(4,128)} %get-tuple-element.147), channel_id=1, source_target_pairs={{0,16},{16,32},{32,48},{48,64},{64,80},{80,96},{96,112},{1,17},{17... | collective-permute-start | bytes 417800 | tf_op jit(solution)/shard_map/ppermute | solution.py:26
  288.5 11.3 %all-to-all-start.6 = ((f32[16,426,4]{1,2,0:T(4,128)}), f32[16,426,4]{1,2,0:T(4,128)S(1)}, u32[]{:S(2)}, u32[]{:S(2)}) async-start(f32[16,426,4]{1,2,0:T(4,128)} %bitcast.33), calls=%async_computation.6 | async-start | bytes 262144 | tf_op jit(solution)/shard_map/all_to_all | solution.py:36
  294.7 14.5 %collective-permute-start.21 = (f32[64,4,136]{2,1,0:T(4,128)}, f32[64,4,136]{2,1,0:T(4,128)}, u32[]{:S(2)}, u32[]{:S(2)}) collective-permute-start(f32[64,4,136]{2,1,0:T(4,128)} %get-tuple-element.146), channel_id=1, source_target_pairs={{16,0},{32,16},{48,32},{64,48},{80,64},{96,80},{112,96},{17,1},{33... | collective-permute-start | bytes 417800 | tf_op jit(solution)/shard_map/ppermute | solution.py:26
  300.5 15.9 %all-to-all-start.7 = ((f32[8,426,4]{1,2,0:T(4,128)}), f32[8,426,4]{1,2,0:T(4,128)S(1)}, u32[]{:S(2)}, u32[]{:S(2)}) async-start(f32[8,426,4]{1,2,0:T(4,128)} %broadcast_in_dim.26), calls=%async_computation.7 | async-start | bytes 131072 | tf_op jit(solution)/shard_map/all_to_all | solution.py:42
  311.4 19.1 %collective-permute-start.23 = (f32[64,16,4]{2,1,0:T(8,128)}, f32[64,16,4]{2,1,0:T(8,128)S(1)}, u32[]{:S(2)}, u32[]{:S(2)}) collective-permute-start(f32[64,16,4]{2,1,0:T(8,128)} %get-tuple-element.161), channel_id=1, source_target_pairs={{1,0},{2,1},{3,2},{4,3},{5,4},{6,5},{7,6},{8,7},{9,8},{10,9},{11,1... | collective-permute-start | bytes 49160 | tf_op jit(solution)/shard_map/ppermute | solution.py:26
  314.5 12.7 %collective-permute-start.22 = (f32[64,16,4]{2,1,0:T(8,128)S(1)}, f32[64,16,4]{2,1,0:T(8,128)}, u32[]{:S(2)}, u32[]{:S(2)}) collective-permute-start(f32[64,16,4]{2,1,0:T(8,128)S(1)} %get-tuple-element.162), channel_id=1, source_target_pairs={{0,1},{1,2},{2,3},{3,4},{4,5},{5,6},{6,7},{7,8},{8,9},{9,10},{10,1... | collective-permute-start | bytes 49160 | tf_op jit(solution)/shard_map/ppermute | solution.py:26
  317.9 24.4 %all-to-all-start.8 = ((f32[16,426,4]{1,2,0:T(4,128)}), f32[16,426,4]{1,2,0:T(4,128)S(1)}, u32[]{:S(2)}, u32[]{:S(2)}) async-start(f32[16,426,4]{1,2,0:T(4,128)} %broadcast_in_dim.27), calls=%async_computation.8 | async-start | bytes 262144 | tf_op jit(solution)/shard_map/all_to_all | solution.py:42
where the time goes:
time: 348 us; the launch traced here: 343 us
  starting transfers between devices  128 us (37%)
  matrix products  84.1 us (24%)
  local copies, waits for them, and re-layouts  69.4 us (20%)
  waiting for transfers between devices  36.6 us (11%)
  other arithmetic  22.5 us (6%)
    ppermute x12, starting transfers between devices, shifted(): return lax.ppermute(block, axis, route)  38.8 us
    scatter-add x3, local copies, waits for them, and re-layouts, on_device(): grad_abund = grad_abund.at[:, :, width - radius:].add(from_right)  31.9 us
    all_to_all x6, starting transfers between devices, from_everyone(): return lax.all_to_all(copies, axis, split_axis=0, concat_axis=0, tiled=True)  31.1 us
    dot_general x27, matrix products, on_device(): lax.dot_general(grad_blur, forward_bands[row_shift], (((2,), (1,)), ((),...  27.2 us
    dot_general x27, matrix products, on_device(): jnp.dot(padded[:, row_shift:row_shift + height, :], forward_bands[row_shi...  27.1 us
    ppermute x6, starting transfers between devices, padded_2(): lax.ppermute(lax.slice_in_dim(block, 0, width, axis=dim), axis, backward)  25.4 us
    ppermute x12, waiting for transfers between devices, shifted(): return lax.ppermute(block, axis, route)  20.6 us
    all_to_all x3, starting transfers between devices, sent_and_summed(): blocks = lax.all_to_all(cut_along(x, dim, devices), axis, 0, 0, tiled=True)  18.1 us
  transfers between devices with their start and end apart: 33, of which 14 were waited for; matrix products, arithmetic and copies ran while one was open for 18% of the time, Pallas kernels for 0%

commit v1 on v0

v1 whole, which is shorter than its diff:
```python
import functools

import jax
import jax.numpy as jnp
from jax import lax
from jax.experimental import pallas as pl
from jax.experimental.pallas import tpu as pltpu
from jax.sharding import PartitionSpec as P

MESH = pl.DeviceIdType.MESH
KS = 9
ITERS = 3
BF = jnp.bfloat16
F32 = jnp.float32
H, W, C = 16, 128, 64
PAIRS = H // 2
EXT = PAIRS + 4
HALF = 216
ROWS = 256


def split(x):
    hi = x.astype(BF)
    return hi, (x - hi.astype(F32)).astype(BF)


def mm(a, b):
    return jnp.dot(a, b, preferred_element_type=F32)


def mm_nt(a, b):
    return lax.dot_general(a, b, (((1,), (1,)), ((), ())), preferred_element_type=F32)


def iota(shape, dim):
    return lax.broadcasted_iota(jnp.int32, shape, dim)


def kernel(
    nr, nc, bands,
    obs_hbm, bend_ref, a_hbm, m_ref, kern_ref, fam_ref,
    out_ref, mout_ref,
    obs_v, a_stage, bend_v, s_main, s_strip, a_main, a_strip, a_hi, a_lo,
    r_up, r_dn, r_one, r_side,
    w_hi, w_lo, wt_hi, wt_lo, fe_hi, fe_lo, as_hi, as_lo,
    bb, g_v, g_hi, g_lo, gc_v, gacc, m_lhs, mt_lhs, q_sel,
    gp, rs_buf, b_src, b_buf, mp,
    in_sem, ex_s, ex_r, rs_s, rs_r, b_s, b_r, c_s, c_r,
):
    r = lax.axis_index("rows")
    c = lax.axis_index("cols")
    has_up, has_dn = r > 0, r < nr - 1
    has_l, has_r = c > 0, c < nc - 1
    rch = ROWS // nc
    npix = float(nr * nc * H * W)

    a_cp = [
        pltpu.make_async_copy(
            a_hbm.at[:, h, :], a_stage.at[h // 2, :, pl.ds((h % 2) * W, W)], in_sem.at[0, h]
        )
        for h in range(H)
    ]
    full = bands // 8 * 8
    tail = bands - full
    o_cp = [
        pltpu.make_async_copy(
            obs_hbm.at[pl.ds(src, size), h, :],
            obs_v.at[h // 2, pl.ds(dst, size), pl.ds((h % 2) * W, W)],
            in_sem.at[k, h],
        )
        for h in range(H)
        for k, src, dst, size in ((1, 0, 0, full), (2, bands - 8, full, 8))
    ]
    for cp in a_cp:
        cp.start()
    for cp in o_cp:
        cp.start()

    barrier = pltpu.get_barrier_semaphore()

    def greet(dr, dc):
        pl.semaphore_signal(barrier, inc=1, device_id=(dr, dc), device_id_type=MESH)

    @pl.loop(1, nc)
    def _(j):
        greet(r, lax.rem(c + j, nc))

    @pl.loop(1, nr)
    def _(j):
        greet(lax.rem(r + j, nr), c)

    corners = (
        (has_up & has_l, -1, -1), (has_up & has_r, -1, 1),
        (has_dn & has_l, 1, -1), (has_dn & has_r, 1, 1),
    )
    for cond, dr, dc in corners:
        @pl.when(cond)
        def _(dr=dr, dc=dc):
            greet(r + dr, c + dc)

    def ex(it):
        up, dn = lax.max(r - 1, 0), lax.min(r + 1, nr - 1)
        lf, rt = lax.max(c - 1, 0), lax.min(c + 1, nc - 1)

        def cp(k, src, dst, dr, dc):
            return pltpu.make_async_remote_copy(
                src_ref=src, dst_ref=dst, send_sem=ex_s.at[it, k], recv_sem=ex_r.at[it, k],
                device_id=(dr, dc), device_id_type=MESH,
            )

        top, bot = s_strip.at[it, 0], s_strip.at[it, 2]
        return (
            (has_dn, has_up, cp(0, s_main.at[it, pl.ds(EXT - 4, 4)], r_up.at[it], dn, c)),
            (has_up, has_dn, cp(1, s_main.at[it, pl.ds(0, 4)], r_dn.at[it], up, c)),
            (has_dn, has_up, cp(2, bot, r_one.at[it, 0], dn, c)),
            (has_up, has_dn, cp(3, top, r_one.at[it, 1], up, c)),
            (has_r, has_l, cp(4, s_strip.at[it], r_side.at[it, 0], r, rt)),
            (has_l, has_r, cp(5, s_strip.at[it], r_side.at[it, 1], r, lf)),
            (has_dn & has_r, has_up & has_l, cp(6, bot, r_one.at[it, 2], dn, rt)),
            (has_dn & has_l, has_up & has_r, cp(7, bot, r_one.at[it, 3], dn, lf)),
            (has_up & has_r, has_dn & has_l, cp(8, top, r_one.at[it, 4], up, rt)),
            (has_up & has_l, has_dn & has_r, cp(9, top, r_one.at[it, 5], up, lf)),
        )

    def ex_start(it):
        for send, _, cp in ex(it):
            @pl.when(send)
            def _(cp=cp):
                cp.start()

    def ex_wait_recv(it):
        for _, recv, cp in ex(it):
            @pl.when(recv)
            def _(cp=cp):
                cp.wait_recv()

    def ex_wait_send(it):
        for send, _, cp in ex(it):
            @pl.when(send)
            def _(cp=cp):
                cp.wait_send()

    @pl.when(jnp.logical_not(has_up))
    def _():
        r_up[...] = jnp.zeros_like(r_up)
        r_one[:, 0] = jnp.zeros((4, C, W), F32)

    @pl.when(jnp.logical_not(has_dn))
    def _():
        r_dn[...] = jnp.zeros_like(r_dn)
        r_one[:, 1] = jnp.zeros((4, C, W), F32)

    @pl.when(jnp.logical_not(has_l))
    def _():
        r_side[:, 0] = jnp.zeros((4, 3, C, W), F32)

    @pl.when(jnp.logical_not(has_r))
    def _():
        r_side[:, 1] = jnp.zeros((4, 3, C, W), F32)

    for k, (cond, _, _) in enumerate(corners):
        @pl.when(jnp.logical_not(cond))
        def _(k=k):
            r_one[:, 2 + k] = jnp.zeros((4, C, W), F32)

    lane = iota((C, W), 1)
    edge_lane = (lane < 4) | (lane >= W - 4)

    zero_pair = jnp.zeros((C, 2 * W), F32)
    for i in (0, 1, EXT - 2, EXT - 1):
        s_main[0, i] = zero_pair
    a_main[...] = jnp.zeros_like(a_main)
    a_strip[...] = jnp.zeros_like(a_strip)
    for cp in a_cp:
        cp.wait()
    for i in range(PAIRS):
        s_main[0, i + 2] = a_stage[i] * (-2.0)
    for t in range(3):
        acc = jnp.zeros((C, W), F32)
        for q in range(8):
            h = 8 * t + q - 4
            if 0 <= h < H:
                row = s_main[0, h // 2 + 2, :, (h % 2) * W:(h % 2 + 1) * W]
                moved = pltpu.roll(row, (16 * q + 8) % W, 1)
                acc = jnp.where((lane >= 16 * q + 4) & (lane < 16 * q + 12), moved, acc)
        s_strip[0, t] = acc

    pl.semaphore_wait(barrier, nc - 1 + nr - 1 + sum(k[0].astype(jnp.int32) for k in corners))
    ex_start(0)

    fam = fam_ref[0, 0]
    row_i, col_i = iota((W, W), 0), iota((W, W), 1)
    zero_blk = jnp.zeros((W, W), BF)
    w_hi[...] = jnp.zeros_like(w_hi)
    w_lo[...] = jnp.zeros_like(w_lo)
    wt_hi[...] = jnp.zeros_like(wt_hi)
    wt_lo[...] = jnp.zeros_like(wt_lo)
    for u in range(KS):
        for diff, hi_ref, lo_ref, flip in (
            (row_i - col_i + 4, w_hi, w_lo, False),
            (col_i - row_i + 4, wt_hi, wt_lo, True),
        ):
            band = jnp.zeros((W, W), F32)
            for v in range(KS):
                band = jnp.where(diff == v, kern_ref[fam, u, v], band)
            hi, lo = split(band)
            for d in range(5):
                for i in range(2):
                    for j in range(2):
                        if 2 * d + i - j == u:
                            a, b = (j, i) if flip else (i, j)
                            sl = (d, pl.ds(a * W, W), pl.ds(b * W, W))
                            hi_ref[sl] = hi
                            lo_ref[sl] = lo

    def table(idx):
        def step(k, acc):
            return jnp.where(idx == k, kern_ref[fam, k // KS, lax.rem(k, KS)], acc)
        return lax.fori_loop(0, KS * KS, step, jnp.zeros((W, W), F32))

    def index(u, v, ok):
        good = ok & (u >= 0) & (u < KS) & (v >= 0) & (v < KS)
        return jnp.where(good, u * KS + v, -1)

    def strip_x(m):
        return jnp.where(m < 4, 128 + m, jnp.where(m < 8, 120 + m, jnp.where(m < 12, m - 8, m - 16)))

    m_row = row_i & 15
    cw = col_i & 7
    w_out = jnp.where(cw < 4, 124 + cw, cw - 4)
    for t in range(3):
        u = 8 * t + (row_i >> 4) - (col_i >> 3)
        v = strip_x(m_row) - w_out + 4
        fe = table(index(u, v, (m_row < 4) | (m_row >= 12)))
        fe_hi[t], fe_lo[t] = split(fe)
    x_in = jnp.where(m_row < 8, 120 + m_row, m_row - 8)
    for t in range(2):
        u = 8 * t + (col_i >> 4) - (row_i >> 4)
        v = strip_x(col_i & 15) - x_in + 4
        as_hi[t], as_lo[t] = split(table(index(u, v, u == u)))

    qr, qc = iota((W, 2 * W), 0), iota((W, 2 * W), 1)
    q_sel[...] = jnp.where(qc == jnp.where(qr < C, qr, qr + C), 1.0, 0.0).astype(BF)
    gacc[...] = jnp.zeros_like(gacc)
    gacc[0:full, 0:C] = m_ref[0:full]
    gacc[2 * HALF - tail:, 0:C] = m_ref[full:bands]
    low = iota((HALF, W), 1) < C
    rows_2 = iota((HALF, W), 0) + HALF
    twice = (rows_2 >= full) & (rows_2 < 2 * HALF - tail)
    md0 = gacc[...] + pltpu.roll(gacc[...], C, 1)
    mp[0, 0:HALF] = jnp.where(low, md0[0:HALF], md0[HALF:])
    mp[0, HALF:ROWS] = jnp.zeros((ROWS - HALF, W), F32)
    gp[:, HALF:ROWS] = jnp.zeros((ITERS, ROWS - HALF, W), F32)
    for h in range(H):
        bend_v[h // 2, :, (h % 2) * W:(h % 2 + 1) * W] = jnp.broadcast_to(
            bend_ref[h:h + 1, :], (8, W)
        )
    g_hi[...] = jnp.zeros_like(g_hi)
    g_lo[...] = jnp.zeros_like(g_lo)

    def spectra_of(k):
        x = mp[k, 0:HALF]
        y = pltpu.roll(x, C, 1)
        return jnp.where(low, x, y), jnp.where(low, y, x)

    def set_spectra(k):
        a, b = spectra_of(k)
        for x, lo_row in ((a, 0), (b, HALF)):
            hi, lo = split(x * (1.0 / C))
            m_lhs[lo_row:lo_row + HALF, 0:W] = hi.astype(F32)
            m_lhs[lo_row:lo_row + HALF, W:] = lo.astype(F32)
        mt_lhs[...] = mm_nt(q_sel[...], m_lhs[...].astype(BF)).astype(BF)

    set_spectra(0)
    for cp in o_cp:
        cp.wait()

    def rs_sum_copies(g):
        whole = rs_buf.at[g, pl.ds(0, nc - 1)]
        return pltpu.make_async_remote_copy(
            src_ref=whole, dst_ref=whole, send_sem=rs_s.at[g], recv_sem=rs_r.at[g],
            device_id=(r, lax.rem(c + 1, nc)), device_id_type=MESH,
        )

    def b_sum_copies(g):
        whole = b_buf.at[g, pl.ds(0, nr - 1)]
        return pltpu.make_async_remote_copy(
            src_ref=whole, dst_ref=whole, send_sem=b_s.at[g], recv_sem=b_r.at[g],
            device_id=(lax.rem(r + 1, nr), c), device_id_type=MESH,
        )

    def c_sum_copies(g):
        whole = mp.at[g + 1, pl.ds(0, ROWS - rch)]
        return pltpu.make_async_remote_copy(
            src_ref=whole, dst_ref=whole, send_sem=c_s.at[g], recv_sem=c_r.at[g],
            device_id=(r, lax.rem(c + 1, nc)), device_id_type=MESH,
        )

    mine = pl.ds(pl.multiple_of(c * rch, rch), rch)

    def rs_start(g):
        rs_buf[g, c] = gp[g, mine]

        @pl.loop(1, nc)
        def _(j):
            t = lax.rem(c + j, nc)
            pltpu.make_async_remote_copy(
                src_ref=gp.at[g, pl.ds(pl.multiple_of(t * rch, rch), rch)],
                dst_ref=rs_buf.at[g, c], send_sem=rs_s.at[g], recv_sem=rs_r.at[g],
                device_id=(r, t), device_id_type=MESH,
            ).start()

    def b_start(g):
        rs_sum_copies(g).wait_recv()
        total = rs_buf[g, 0]
        for j in range(1, nc):
            total = total + rs_buf[g, j]
        b_src[g] = total
        b_buf[g, r] = total

        @pl.loop(1, nr)
        def _(j):
            pltpu.make_async_remote_copy(
                src_ref=b_src.at[g], dst_ref=b_buf.at[g, r],
                send_sem=b_s.at[g], recv_sem=b_r.at[g],
                device_id=(lax.rem(r + j, nr), c), device_id_type=MESH,
            ).start()

    def c_start(g):
        b_sum_copies(g).wait_recv()
        total = b_buf[g, 0]
        for j in range(1, nr):
            total = total + b_buf[g, j]
        mp[g + 1, mine] = jnp.maximum(mp[g, mine] - 40.0 * (total / npix), 0.0)

        @pl.loop(1, nc)
        def _(j):
            pltpu.make_async_remote_copy(
                src_ref=mp.at[g + 1, mine], dst_ref=mp.at[g + 1, mine],
                send_sem=c_s.at[g], recv_sem=c_r.at[g],
                device_id=(r, lax.rem(c + j, nc)), device_id_type=MESH,
            ).start()

    lane_m = lane & 15
    lane_q = lane >> 4

    def update(it):
        xs = []
        for t in range(3):
            left, right = r_side[it, 0, t], r_side[it, 1, t]
            if t == 0:
                left, right = left + r_one[it, 2], right + r_one[it, 3]
            if t == 2:
                left, right = left + r_one[it, 4], right + r_one[it, 5]
            x = jnp.where(lane_m >= 8, pltpu.roll(left, 8, 1), pltpu.roll(right, W - 8, 1))
            xs.append(x)
            total = s_strip[it, t] + x
            ok = ((lane_m < 4) & has_r) | ((lane_m >= 12) & has_l)
            if t == 0:
                total = total + r_one[it, 0]
                ok = ok & ((lane_q >= 4) | has_up)
            if t == 2:
                total = total + r_one[it, 1]
                ok = ok & ((lane_q < 4) | has_dn)
            a_strip[t] = jnp.maximum(a_strip[t] - 0.5 * jnp.where(ok, total, 0.0), 0.0)
        for i in range(EXT):
            for j in range(2):
                e = 2 * i + j
                sl = slice(j * W, (j + 1) * W)
                total = s_main[it, i, :, sl]
                if i < 4:
                    total = total + r_up[it, i, :, sl]
                if i >= EXT - 4:
                    total = total + r_dn[it, i - (EXT - 4), :, sl]
                moved = pltpu.roll(xs[e // 8], (120 - 16 * (e % 8)) % W, 1)
                total = total + jnp.where(edge_lane, moved, 0.0)
                if e < 4:
                    total = jnp.where(has_up, total, 0.0)
                if e >= H + 4:
                    total = jnp.where(has_dn, total, 0.0)
                new = jnp.maximum(a_main[i, :, sl] - 0.5 * total, 0.0)
                a_main[i, :, sl] = new
                hi, lo = split(new)
                a_hi[i, :, sl] = hi
                a_lo[i, :, sl] = lo

    def blur():
        edge = jnp.zeros((C, W), F32)
        for t in range(3):
            hi, lo = split(a_strip[t])
            edge = edge + mm(hi, fe_hi[t]) + mm(lo, fe_hi[t]) + mm(hi, fe_lo[t])
        for half in range(2):
            base = half * 4
            acc = None
            for d in range(5):
                hi = a_hi[base + d:base + d + 4].reshape(4 * C, 2 * W)
                lo = a_lo[base + d:base + d + 4].reshape(4 * C, 2 * W)
                part = mm(hi, w_hi[d]) + mm(lo, w_hi[d]) + mm(hi, w_lo[d])
                acc = part if acc is None else acc + part
            for k in range(4):
                for j in range(2):
                    h = 2 * (base + k) + j
                    moved = pltpu.roll(edge, (-8 * h - 4) % W, 1)
                    val = acc[k * C:(k + 1) * C, j * W:(j + 1) * W]
                    val = val + jnp.where(edge_lane, moved, 0.0)
                    hi, lo = split(val)
                    bb[base + k, 0:C, j * W:(j + 1) * W] = hi
                    bb[base + k, C:, j * W:(j + 1) * W] = lo

    def spectral():
        gacc[...] = jnp.zeros_like(gacc)

        @pl.loop(0, PAIRS)
        def _(p):
            both = bb[p]
            lin = mm(m_lhs[...].astype(BF), jnp.concatenate([both, both], axis=0))
            t = lin * bend_v[p, 0:1, :]
            a = 1.0 + t
            resid = lin * a - obs_v[p]
            hi, lo = split(resid * (a + t))
            gacc[...] += mm_nt(hi, both) + mm_nt(lo, both)
            part = mm(mt_lhs[...], hi) + mm(mt_lhs[...], lo)
            g = part[0:C] + part[C:]
            g_v[p] = g
            ghi, glo = split(g)
            g_hi[p + 4] = ghi
            g_lo[p + 4] = glo

    def pack_grad(it):
        g = gacc[...]
        g = (g + pltpu.roll(g, C, 1)) * (1.0 / C)
        second = jnp.where(twice, 0.0, g[HALF:])
        gp[it, 0:HALF] = jnp.where(low, g[0:HALF], second)

    def adjoint(it):
        for t in range(2):
            acc = jnp.zeros((C, W), F32)
            for q in range(8):
                h = 8 * t + q
                row = g_v[h // 2, :, (h % 2) * W:(h % 2 + 1) * W]
                acc = jnp.where(lane_q == q, pltpu.roll(row, (16 * q + 8) % W, 1), acc)
            gc_v[t] = acc
        h0, l0 = split(gc_v[0])
        h1, l1 = split(gc_v[1])

        def strip(hi, lo, t):
            return mm(hi, as_hi[t]) + mm(lo, as_hi[t]) + mm(hi, as_lo[t])

        s_strip[it, 0] = strip(h0, l0, 0)
        s_strip[it, 1] = strip(h0, l0, 1) + strip(h1, l1, 0)
        s_strip[it, 2] = strip(h1, l1, 1)
        for part in (0, 2, 1):
            base = 4 * part
            acc = None
            for d in range(5):
                if (part == 0 and d == 4) or (part == 2 and d == 0):
                    continue
                lo_row = base - d + 4
                hi = g_hi[lo_row:lo_row + 4].reshape(4 * C, 2 * W)
                lo = g_lo[lo_row:lo_row + 4].reshape(4 * C, 2 * W)
                term = mm(hi, wt_hi[d]) + mm(lo, wt_hi[d]) + mm(hi, wt_lo[d])
                acc = term if acc is None else acc + term
            for k in range(4):
                s_main[it, base + k] = acc[k * C:(k + 1) * C]

    @pl.loop(0, ITERS + 1)
    def _(it):
        @pl.when(it > 0)
        def _():
            b_start(it - 1)

        ex_wait_recv(it)
        update(it)

        @pl.when(it > 0)
        def _():
            c_start(it - 1)

        @pl.when(it < ITERS)
        def _():
            blur()

        @pl.when(it > 0)
        def _():
            c_sum_copies(it - 1).wait_recv()

        @pl.when((it > 0) & (it < ITERS))
        def _():
            set_spectra(it)

        @pl.when(it < ITERS)
        def _():
            spectral()
            pack_grad(it)
            rs_start(it)
            adjoint(it + 1)
            ex_start(it + 1)

        ex_wait_send(it)

        @pl.when(it > 0)
        def _():
            rs_sum_copies(it - 1).wait_send()
            b_sum_copies(it - 1).wait_send()
            c_sum_copies(it - 1).wait_send()

    for h in range(H):
        out_ref[h] = a_main[h // 2 + 2, :, (h % 2) * W:(h % 2 + 1) * W]
    a, b = spectra_of(ITERS)
    mout_ref[0:HALF] = a[:, 0:C]
    mout_ref[HALF:full] = b[0:full - HALF, 0:C]
    mout_ref[full:bands] = b[HALF - tail:, 0:C]


def solution(mesh):
    nr, nc = mesh.shape["rows"], mesh.shape["cols"]
    rch = ROWS // nc

    def on_device(observed, nonlin, abundance, spectra, kernels, tile_family):
        bands = observed.shape[0]
        vm = pltpu.VMEM
        dma = pltpu.SemaphoreType.DMA
        scratch = [
            vm((PAIRS, 2 * HALF, 2 * W), F32), vm((PAIRS, C, 2 * W), F32), vm((PAIRS, 8, 2 * W), F32),
            vm((4, EXT, C, 2 * W), F32), vm((4, 3, C, W), F32),
            vm((EXT, C, 2 * W), F32), vm((3, C, W), F32), vm((EXT, C, 2 * W), BF), vm((EXT, C, 2 * W), BF),
            vm((4, 4, C, 2 * W), F32), vm((4, 4, C, 2 * W), F32), vm((4, 6, C, W), F32),
            vm((4, 2, 3, C, W), F32),
            vm((5, 2 * W, 2 * W), BF), vm((5, 2 * W, 2 * W), BF),
            vm((5, 2 * W, 2 * W), BF), vm((5, 2 * W, 2 * W), BF),
            vm((3, W, W), BF), vm((3, W, W), BF), vm((2, W, W), BF), vm((2, W, W), BF),
            vm((PAIRS, 2 * C, 2 * W), BF), vm((PAIRS, C, 2 * W), F32),
            vm((EXT + 4, C, 2 * W), BF), vm((EXT + 4, C, 2 * W), BF), vm((2, C, W), F32),
            vm((2 * HALF, W), F32), vm((2 * HALF, 2 * W), F32), vm((W, 2 * HALF), BF), vm((W, 2 * W), BF),
            vm((ITERS, ROWS, W), F32), vm((ITERS, nc, rch, W), F32), vm((ITERS, rch, W), F32),
            vm((ITERS, nr, rch, W), F32), vm((ITERS + 1, ROWS, W), F32),
            dma((3, H)), dma((4, 10)), dma((4, 10)),
            dma((ITERS,)), dma((ITERS,)), dma((ITERS,)), dma((ITERS,)), dma((ITERS,)), dma((ITERS,)),
        ]
        any_spec = pl.BlockSpec(memory_space=pl.ANY)
        vspec = pl.BlockSpec(memory_space=pltpu.VMEM)
        sspec = pl.BlockSpec(memory_space=pltpu.SMEM)
        out, m_out = pl.pallas_call(
            functools.partial(kernel, nr, nc, bands),
            out_shape=(
                jax.ShapeDtypeStruct((H, C, W), F32),
                jax.ShapeDtypeStruct((bands, C), F32),
            ),
            in_specs=[any_spec, vspec, any_spec, vspec, sspec, sspec],
            out_specs=(vspec, vspec),
            scratch_shapes=scratch,
            compiler_params=pltpu.CompilerParams(collective_id=0, has_side_effects=True),
            name="unmix",
        )(observed, nonlin, abundance, spectra, kernels, tile_family)
        return jnp.transpose(out, (1, 0, 2)), m_out

    placed = (
        P(None, "rows", "cols"), P("rows", "cols"), P(None, "rows", "cols"),
        P(), P(), P("rows", "cols"),
    )
    return jax.shard_map(
        on_device, mesh=mesh, in_specs=placed,
        out_specs=(P(None, "rows", "cols"), P()), check_vma=False,
    )
```

time: 348 us -> 105 us (0.30)
  the two profiles are of different devices: /device:TPU:98 before, /device:TPU:1 now
where the time goes in v1:
time: 105 us
  Pallas kernels  96.5 us (92%)
  local copies, waits for them, and re-layouts  6.98 us (7%)
  between operations  1.29 us (1%)
    pallas_call x1, Pallas kernels, on_device(): pl.pallas_call(functools.partial(kernel, nr, nc, bands), out_shape=(jax.S...  96.5 us
    unnamed x4, local copies, waits for them, and re-layouts  6.98 us

profile of v1, /device:TPU:1, one launch (start us, length us, event | category | flops | bytes accessed | tf_op | source)
XLA Modules:
  0.0 104.8 jit_solution(13594973180698081982)
XLA Ops:
  1.3 1.4 %copy.9.kern_ref = f32[8,9,9]{2,1,0:T(8,128)} copy(f32[8,9,9]{2,0,1:T(8,128)} %param.10) | data formatting | bytes 5184 | tf_op args[4]
  2.7 1.7 %copy.8.m_ref = f32[426,64]{1,0:T(8,128)} copy(f32[426,64]{0,1:T(8,128)} %param.9) | data formatting | bytes 218112 | tf_op args[3]
  4.4 96.5 %unmix.1 = (f32[16,64,128]{2,1,0:T(8,128)}, f32[426,64]{1,0:T(8,128)}) custom-call(f32[426,16,128]{2,1,0:T(8,128)} %obs_hbm.1, f32[16,128]{1,0:T(8,128)} %bend_ref.1, f32[64,16,128]{2,1,0:T(8,128)} %a_hbm.1, f32[426,64]{1,0:T(8,128)} %copy.8.m_ref, f32[8,9,9]{2,1,0:T(8,128)} %copy.9.kern_ref, s32[1,1]{1,0:T(1,128)S(6)} %copy.12.fam_ref), custom_call_target="tpu_custom_call" | custom-call | tf_op jit(solution)/shard_map/unmix/pallas_call | solution.py:543
  100.9 2.1 %copy.10 = f32[64,16,128]{2,1,0:T(8,128)} copy(f32[64,16,128]{2,0,1:T(8,128)} %bitcast.1) | data formatting | bytes 1048576
  103.1 1.7 %copy.11 = f32[426,64]{0,1:T(8,128)} copy(f32[426,64]{1,0:T(8,128)} %get-tuple-element.7) | data formatting | bytes 218112

commit v2 on v1

v2 whole, which is shorter than its diff:
```python
import functools

import jax
import jax.numpy as jnp
from jax import lax
from jax.experimental import pallas as pl
from jax.experimental.pallas import tpu as pltpu
from jax.sharding import PartitionSpec as P

MESH = pl.DeviceIdType.MESH
KS = 9
ITERS = 3
BF = jnp.bfloat16
F32 = jnp.float32
H, W, C = 16, 128, 64
PAIRS = H // 2
EXT = PAIRS + 4
HALF = 216
ROWS = 256


def split(x):
    hi = x.astype(BF)
    return hi, (x - hi.astype(F32)).astype(BF)


def mm(a, b):
    return jnp.dot(a, b, preferred_element_type=F32)


def mm_nt(a, b):
    return lax.dot_general(a, b, (((1,), (1,)), ((), ())), preferred_element_type=F32)


def iota(shape, dim):
    return lax.broadcasted_iota(jnp.int32, shape, dim)


def kernel(
    nr, nc, bands,
    obs_hbm, bend_ref, a_hbm, m_ref, kern_ref, fam_ref,
    out_hbm, mout_ref,
    obs_v, a_stage, bend_v, s_main, s_strip, a_main, a_strip, a3,
    r_up, r_dn, r_one, r_side, v_buf, x_buf,
    w3, wt3, fe3, as3,
    acc_b, bb, wgt_hi, wgt_lo, g_v, g3, gacc, m_lhs, mt_lhs, q_sel, m_t,
    gp, rs_buf, b_src, b_buf, mp,
    in_sem, ex_s, ex_r, rs_s, rs_r, b_s, b_r, c_s, c_r,
):
    r = lax.axis_index("rows")
    c = lax.axis_index("cols")
    has_up, has_dn = r > 0, r < nr - 1
    has_l, has_r = c > 0, c < nc - 1
    rch = ROWS // nc
    npix = float(nr * nc * H * W)

    barrier = pltpu.get_barrier_semaphore()

    def greet(dr, dc):
        pl.semaphore_signal(barrier, inc=1, device_id=(dr, dc), device_id_type=MESH)

    @pl.loop(1, nc)
    def _(j):
        greet(r, lax.rem(c + j, nc))

    @pl.loop(1, nr)
    def _(j):
        greet(lax.rem(r + j, nr), c)

    a_cp = [
        pltpu.make_async_copy(
            a_hbm.at[:, h, :], a_stage.at[h // 2, :, pl.ds((h % 2) * W, W)], in_sem.at[0, h]
        )
        for h in range(H)
    ]
    full = bands // 8 * 8
    tail = bands - full
    o_cp = [
        pltpu.make_async_copy(
            obs_hbm.at[pl.ds(src, size), h, :],
            obs_v.at[h // 2, pl.ds(dst, size), pl.ds((h % 2) * W, W)],
            in_sem.at[k, h],
        )
        for h in range(H)
        for k, src, dst, size in ((1, 0, 0, full), (2, bands - 8, full, 8))
    ]
    for cp in a_cp:
        cp.start()
    for cp in o_cp:
        cp.start()

    def ex(it):
        up, dn = lax.max(r - 1, 0), lax.min(r + 1, nr - 1)
        lf, rt = lax.max(c - 1, 0), lax.min(c + 1, nc - 1)

        def cp(k, src, dst, dr, dc):
            return pltpu.make_async_remote_copy(
                src_ref=src, dst_ref=dst, send_sem=ex_s.at[it, k], recv_sem=ex_r.at[it, k],
                device_id=(dr, dc), device_id_type=MESH,
            )

        over, halo = it > 0, it < ITERS
        side = (
            (has_r, has_l, cp(4, s_strip.at[it], r_side.at[it, 0], r, rt)),
            (has_l, has_r, cp(5, s_strip.at[it], r_side.at[it, 1], r, lf)),
        )
        rows_a = (
            (has_dn & over, has_up & over,
             cp(0, s_main.at[it, pl.ds(EXT - 2, 2)], r_up.at[it, pl.ds(2, 2)], dn, c)),
            (has_up & over, has_dn & over,
             cp(1, s_main.at[it, pl.ds(0, 2)], r_dn.at[it, pl.ds(0, 2)], up, c)),
        )
        rows_b = (
            (has_dn & halo, has_up & halo,
             cp(6, s_main.at[it, pl.ds(EXT - 4, 2)], r_up.at[it, pl.ds(0, 2)], dn, c)),
            (has_up & halo, has_dn & halo,
             cp(7, s_main.at[it, pl.ds(2, 2)], r_dn.at[it, pl.ds(2, 2)], up, c)),
        )
        ends = (
            (has_dn, has_up, cp(2, v_buf.at[it, 1], r_one.at[it, 0], dn, c)),
            (has_up, has_dn, cp(3, v_buf.at[it, 0], r_one.at[it, 1], up, c)),
        )
        return side, rows_a, rows_b, ends

    def start(copies):
        for send, _, cp in copies:
            @pl.when(send)
            def _(cp=cp):
                cp.start()

    def wait_recv(copies):
        for _, recv, cp in copies:
            @pl.when(recv)
            def _(cp=cp):
                cp.wait_recv()

    def wait_send(copies):
        for send, _, cp in copies:
            @pl.when(send)
            def _(cp=cp):
                cp.wait_send()

    @pl.when(jnp.logical_not(has_up))
    def _():
        r_up[...] = jnp.zeros_like(r_up)
        r_one[:, 0] = jnp.zeros((4, C, W), F32)

    @pl.when(jnp.logical_not(has_dn))
    def _():
        r_dn[...] = jnp.zeros_like(r_dn)
        r_one[:, 1] = jnp.zeros((4, C, W), F32)

    @pl.when(jnp.logical_not(has_l))
    def _():
        r_side[:, 0] = jnp.zeros((4, 3, C, W), F32)

    @pl.when(jnp.logical_not(has_r))
    def _():
        r_side[:, 1] = jnp.zeros((4, 3, C, W), F32)

    @pl.when(has_up)
    def _():
        r_up[0, 2:4] = jnp.zeros((2, C, 2 * W), F32)

    @pl.when(has_dn)
    def _():
        r_dn[0, 0:2] = jnp.zeros((2, C, 2 * W), F32)

    lane = iota((C, W), 1)
    edge_lane = (lane < 4) | (lane >= W - 4)

    zero_pair = jnp.zeros((C, 2 * W), F32)
    for i in (0, 1, EXT - 2, EXT - 1):
        s_main[0, i] = zero_pair
    a_main[...] = jnp.zeros_like(a_main)
    a_strip[...] = jnp.zeros_like(a_strip)
    for cp in a_cp:
        cp.wait()
    for i in range(PAIRS):
        s_main[0, i + 2] = a_stage[i] * (-2.0)
    for t in range(3):
        acc = jnp.zeros((C, W), F32)
        for q in range(8):
            h = 8 * t + q - 4
            if 0 <= h < H:
                row = s_main[0, h // 2 + 2, :, (h % 2) * W:(h % 2 + 1) * W]
                moved = pltpu.roll(row, (16 * q + 8) % W, 1)
                acc = jnp.where((lane >= 16 * q + 4) & (lane < 16 * q + 12), moved, acc)
        s_strip[0, t] = acc

    fam = fam_ref[0, 0]
    row_i, col_i = iota((W, W), 0), iota((W, W), 1)
    for ref in (w3, wt3):
        for d, i, j in ((0, 0, 1), (4, 1, 0)):
            i, j = (j, i) if ref is wt3 else (i, j)
            for k in range(3):
                ref[d, (2 * k + i) * W:(2 * k + i + 1) * W, j * W:(j + 1) * W] = jnp.zeros((W, W), BF)
    for u in range(KS):
        for diff, ref, flip in ((row_i - col_i + 4, w3, False), (col_i - row_i + 4, wt3, True)):
            band = jnp.zeros((W, W), F32)
            for v in range(KS):
                band = jnp.where(diff == v, kern_ref[u, fam, v], band)
            hi, lo = split(band)
            for d in range(5):
                for i in range(2):
                    for j in range(2):
                        if 2 * d + i - j == u:
                            a, b = (j, i) if flip else (i, j)
                            for k, val in ((0, hi), (1, hi), (2, lo)):
                                ref[d, (2 * k + a) * W:(2 * k + a + 1) * W, b * W:(b + 1) * W] = val

    def table(idx):
        def step(u, acc):
            for v in range(KS):
                acc = jnp.where(idx == u * KS + v, kern_ref[u, fam, v], acc)
            return acc
        hi, lo = split(lax.fori_loop(0, KS, step, jnp.zeros((W, W), F32)))
        return jnp.concatenate([hi, hi, lo], axis=0)

    def index(u, v, ok):
        good = ok & (u >= 0) & (u < KS) & (v >= 0) & (v < KS)
        return jnp.where(good, u * KS + v, -1)

    def strip_x(m):
        return jnp.where(m < 4, 128 + m, jnp.where(m < 8, 120 + m, jnp.where(m < 12, m - 8, m - 16)))

    m_row = row_i & 15
    cw = col_i & 7
    w_out = jnp.where(cw < 4, 124 + cw, cw - 4)
    for t in range(3):
        u = 8 * t + (row_i >> 4) - (col_i >> 3)
        v = strip_x(m_row) - w_out + 4
        fe3[t] = table(index(u, v, (m_row < 4) | (m_row >= 12)))
    x_in = jnp.where(m_row < 8, 120 + m_row, m_row - 8)
    for t in range(2):
        u = 8 * t + (col_i >> 4) - (row_i >> 4)
        v = strip_x(col_i & 15) - x_in + 4
        as3[t] = table(index(u, v, u == u))

    pl.semaphore_wait(barrier, nc - 1 + nr - 1)
    for part in ex(0)[:3]:
        start(part)


    qr, qc = iota((W, 2 * W), 0), iota((W, 2 * W), 1)
    q_sel[...] = jnp.where(qc == jnp.where(qr < C, qr, qr + C), 1.0, 0.0).astype(BF)
    m_t[...] = jnp.zeros_like(m_t)
    m_t[0:C, 0:bands] = m_ref[...]
    m_rows = jnp.transpose(m_t[...])
    gacc[0:full] = m_rows[0:full]
    gacc[full:] = jnp.zeros((2 * HALF - full, W), F32)
    gacc[2 * HALF - tail:] = m_rows[full:bands]
    low = iota((HALF, W), 1) < C
    rows_2 = iota((HALF, W), 0) + HALF
    twice = (rows_2 >= full) & (rows_2 < 2 * HALF - tail)
    md0 = gacc[...] + pltpu.roll(gacc[...], C, 1)
    mp[0, 0:HALF] = jnp.where(low, md0[0:HALF], md0[HALF:])
    mp[0, HALF:ROWS] = jnp.zeros((ROWS - HALF, W), F32)
    gp[:, HALF:ROWS] = jnp.zeros((ITERS, ROWS - HALF, W), F32)
    for h in range(H):
        bend_v[h // 2, :, (h % 2) * W:(h % 2 + 1) * W] = jnp.broadcast_to(
            bend_ref[h:h + 1, :], (8, W)
        )

    def spectra_of(k):
        x = mp[k, 0:HALF]
        y = pltpu.roll(x, C, 1)
        return jnp.where(low, x, y), jnp.where(low, y, x)

    def set_spectra(k):
        a, b = spectra_of(k)
        hi, lo = split(jnp.concatenate([a, b], axis=0) * (1.0 / C))
        m_lhs[:, 0:W] = hi
        m_lhs[:, W:] = lo
        mt_lhs[...] = mm_nt(q_sel[...], m_lhs[...]).astype(BF)

    set_spectra(0)
    for cp in o_cp:
        cp.wait()

    def rs_sum_copies(g):
        whole = rs_buf.at[g, pl.ds(0, nc - 1)]
        return pltpu.make_async_remote_copy(
            src_ref=whole, dst_ref=whole, send_sem=rs_s.at[g], recv_sem=rs_r.at[g],
            device_id=(r, lax.rem(c + 1, nc)), device_id_type=MESH,
        )

    def b_sum_copies(g):
        whole = b_buf.at[g, pl.ds(0, nr - 1)]
        return pltpu.make_async_remote_copy(
            src_ref=whole, dst_ref=whole, send_sem=b_s.at[g], recv_sem=b_r.at[g],
            device_id=(lax.rem(r + 1, nr), c), device_id_type=MESH,
        )

    def c_sum_copies(g):
        whole = mp.at[g + 1, pl.ds(0, ROWS - rch)]
        return pltpu.make_async_remote_copy(
            src_ref=whole, dst_ref=whole, send_sem=c_s.at[g], recv_sem=c_r.at[g],
            device_id=(r, lax.rem(c + 1, nc)), device_id_type=MESH,
        )

    mine = pl.ds(pl.multiple_of(c * rch, rch), rch)

    def rs_start(g):
        rs_buf[g, c] = gp[g, mine]

        @pl.loop(1, nc)
        def _(j):
            t = lax.rem(c + j, nc)
            pltpu.make_async_remote_copy(
                src_ref=gp.at[g, pl.ds(pl.multiple_of(t * rch, rch), rch)],
                dst_ref=rs_buf.at[g, c], send_sem=rs_s.at[g], recv_sem=rs_r.at[g],
                device_id=(r, t), device_id_type=MESH,
            ).start()

    def b_start(g):
        rs_sum_copies(g).wait_recv()
        total = rs_buf[g, 0]
        for j in range(1, nc):
            total = total + rs_buf[g, j]
        b_src[g] = total
        b_buf[g, r] = total

        @pl.loop(1, nr)
        def _(j):
            pltpu.make_async_remote_copy(
                src_ref=b_src.at[g], dst_ref=b_buf.at[g, r],
                send_sem=b_s.at[g], recv_sem=b_r.at[g],
                device_id=(lax.rem(r + j, nr), c), device_id_type=MESH,
            ).start()

    def c_start(g):
        b_sum_copies(g).wait_recv()
        total = b_buf[g, 0]
        for j in range(1, nr):
            total = total + b_buf[g, j]
        mp[g + 1, mine] = jnp.maximum(mp[g, mine] - 40.0 * (total / npix), 0.0)

        @pl.loop(1, nc)
        def _(j):
            pltpu.make_async_remote_copy(
                src_ref=mp.at[g + 1, mine], dst_ref=mp.at[g + 1, mine],
                send_sem=c_s.at[g], recv_sem=c_r.at[g],
                device_id=(r, lax.rem(c + j, nc)), device_id_type=MESH,
            ).start()

    lane_m = lane & 15
    lane_q = lane >> 4

    def lhs3(x):
        hi, lo = split(x)
        return jnp.concatenate([hi, lo, hi], axis=1)

    halo_lane = (lane_m < 4) | (lane_m >= 12)

    def sides_in(it):
        for t in range(3):
            left, right = r_side[it, 0, t], r_side[it, 1, t]
            x = jnp.where(lane_m >= 8, pltpu.roll(left, 8, 1), pltpu.roll(right, W - 8, 1))
            x_buf[t] = x
            if t != 1:
                v_buf[it, t // 2] = x + jnp.where(halo_lane, s_strip[it, t], 0.0)

    def update(it, t):
        x = x_buf[t]
        if t != 1:
            x = x + r_one[it, t // 2]
        total = s_strip[it, t] + x
        ok = ((lane_m < 4) & has_r) | ((lane_m >= 12) & has_l)
        if t == 0:
            ok = ok & ((lane_q >= 4) | has_up)
        if t == 2:
            ok = ok & ((lane_q < 4) | has_dn)
        a_strip[t] = jnp.maximum(a_strip[t] - 0.5 * jnp.where(ok, total, 0.0), 0.0)
        for i in range(4 * t, 4 * t + 4):
            for j in range(2):
                e = 2 * i + j
                sl = slice(j * W, (j + 1) * W)
                total = s_main[it, i, :, sl]
                if t == 0:
                    total = total + r_up[it, i, :, sl]
                if t == 2:
                    total = total + r_dn[it, i - (EXT - 4), :, sl]
                moved = pltpu.roll(x, (120 - 16 * (e % 8)) % W, 1)
                total = total + jnp.where(edge_lane, moved, 0.0)
                if e < 4:
                    total = jnp.where(has_up, total, 0.0)
                if e >= H + 4:
                    total = jnp.where(has_dn, total, 0.0)
                new = jnp.maximum(a_main[i, :, sl] - 0.5 * total, 0.0)
                a_main[i, :, sl] = new
                hi, lo = split(new)
                a3[i, :, j * W:(j + 1) * W] = hi
                a3[i, :, (2 + j) * W:(3 + j) * W] = lo
                a3[i, :, (4 + j) * W:(5 + j) * W] = hi

    def blocks(x, n):
        return x.reshape(n, C, 2 * W)

    def blur_inner():
        lhs = a3[4:8].reshape(4 * C, 6 * W)
        acc_b[4:8] = blocks(mm(lhs, w3[0]), 4)
        acc_b[0:4] = blocks(mm(lhs, w3[4]), 4)
        for d in (1, 2, 3):
            acc_b[4 - d:8 - d] += blocks(mm(lhs, w3[d]), 4)

    def blur_outer():
        for d in range(5):
            parts = []
            if d < 4:
                parts.append(a3[d:4].reshape((4 - d) * C, 6 * W))
            if d > 0:
                parts.append(a3[8:8 + d].reshape(d * C, 6 * W))
            res = mm(parts[0] if len(parts) == 1 else jnp.concatenate(parts, axis=0), w3[d])
            if d < 4:
                acc_b[0:4 - d] += blocks(res[0:(4 - d) * C], 4 - d)
            if d > 0:
                acc_b[8 - d:8] += blocks(res[(4 - d) * C:], d)
        edge = mm(lhs3(a_strip[0]), fe3[0]) + mm(lhs3(a_strip[1]), fe3[1]) + mm(lhs3(a_strip[2]), fe3[2])
        for p in range(PAIRS):
            for j in range(2):
                h = 2 * p + j
                moved = pltpu.roll(edge, (-8 * h - 4) % W, 1)
                val = acc_b[p, :, j * W:(j + 1) * W] + jnp.where(edge_lane, moved, 0.0)
                hi, lo = split(val)
                bb[p, 0:C, j * W:(j + 1) * W] = hi
                bb[p, C:, j * W:(j + 1) * W] = lo

    def spectral(it):
        gacc[...] = jnp.zeros_like(gacc)

        @pl.loop(0, PAIRS, unroll=PAIRS)
        def _(p):
            both = bb[p]
            lin = mm(m_lhs[...], jnp.concatenate([both, both], axis=0))
            t = lin * bend_v[p, 0:1, :]
            a = 1.0 + t
            resid = lin * a - obs_v[p]
            hi, lo = split(resid * (a + t))
            wgt_hi[p] = hi
            wgt_lo[p] = lo
            gacc[...] += mm_nt(hi, both) + mm_nt(lo, both)

        g = gacc[...]
        g = (g + pltpu.roll(g, C, 1)) * (1.0 / C)
        second = jnp.where(twice, 0.0, g[HALF:])
        gp[it, 0:HALF] = jnp.where(low, g[0:HALF], second)

    def pixel_grad():
        @pl.loop(0, PAIRS, unroll=PAIRS)
        def _(p):
            part = mm(mt_lhs[...], wgt_hi[p]) + mm(mt_lhs[...], wgt_lo[p])
            g = part[0:C] + part[C:]
            g_v[p] = g
            g3[p] = lhs3(g)

    def adjoint_strips(it):
        packed = []
        for t in range(2):
            acc = jnp.zeros((C, W), F32)
            for q in range(8):
                h = 8 * t + q
                row = g_v[h // 2, :, (h % 2) * W:(h % 2 + 1) * W]
                acc = jnp.where(lane_q == q, pltpu.roll(row, (16 * q + 8) % W, 1), acc)
            packed.append(lhs3(acc))
        s_strip[it, 0] = mm(packed[0], as3[0])
        s_strip[it, 1] = mm(packed[0], as3[1]) + mm(packed[1], as3[0])
        s_strip[it, 2] = mm(packed[1], as3[1])

    def adjoint_outer(it):
        for d in (0, 4, 1, 2, 3):
            parts = []
            if d < 4:
                parts.append(g3[0:4 - d].reshape((4 - d) * C, 6 * W))
            if d > 0:
                parts.append(g3[8 - d:8].reshape(d * C, 6 * W))
            res = mm(parts[0] if len(parts) == 1 else jnp.concatenate(parts, axis=0), wt3[d])
            if d == 0:
                s_main[it, 0:4] = blocks(res, 4)
            elif d == 4:
                s_main[it, 8:12] = blocks(res, 4)
            else:
                s_main[it, d:4] += blocks(res[0:(4 - d) * C], 4 - d)
                s_main[it, 8:8 + d] += blocks(res[(4 - d) * C:], d)

    def adjoint_inner(it):
        for d in range(5):
            res = blocks(mm(g3[4 - d:8 - d].reshape(4 * C, 6 * W), wt3[d]), 4)
            if d == 0:
                s_main[it, 4:8] = res
            else:
                s_main[it, 4:8] += res

    def out_copies():
        return [
            pltpu.make_async_copy(
                a_main.at[h // 2 + 2, :, pl.ds((h % 2) * W, W)], out_hbm.at[:, h, :], in_sem.at[0, h]
            )
            for h in range(H)
        ]

    @pl.loop(0, ITERS + 1)
    def _(it):
        side, rows_a, rows_b, ends = ex(it)
        more = it < ITERS

        @pl.when(it > 0)
        def _():
            b_start(it - 1)

        wait_recv(side)
        sides_in(it)
        start(ends)

        @pl.when(it > 0)
        def _():
            start(rows_b)

        update(it, 1)

        @pl.when(more)
        def _():
            blur_inner()

        @pl.when(it > 0)
        def _():
            c_start(it - 1)

        wait_recv(rows_a)
        wait_recv(rows_b)
        wait_recv(ends)
        update(it, 0)
        update(it, 2)

        @pl.when(more)
        def _():
            blur_outer()

        @pl.when(it == ITERS)
        def _():
            for cp in out_copies():
                cp.start()

        @pl.when(it > 0)
        def _():
            c_sum_copies(it - 1).wait_recv()

        @pl.when((it > 0) & more)
        def _():
            set_spectra(it)

        @pl.when(more)
        def _():
            spectral(it)
            rs_start(it)
            pixel_grad()
            adjoint_strips(it + 1)
            next_side, next_rows, _, _ = ex(it + 1)
            start(next_side)
            adjoint_outer(it + 1)
            start(next_rows)
            adjoint_inner(it + 1)

        wait_send(side)
        wait_send(rows_a)
        wait_send(rows_b)
        wait_send(ends)

        @pl.when(it > 0)
        def _():
            rs_sum_copies(it - 1).wait_send()
            b_sum_copies(it - 1).wait_send()
            c_sum_copies(it - 1).wait_send()

    a, b = spectra_of(ITERS)
    gacc[0:HALF] = a
    gacc[HALF:] = b
    last = gacc[2 * HALF - tail:]
    gacc[full:bands] = last
    m_rows_t = jnp.transpose(jnp.concatenate([gacc[...], jnp.zeros((4 * W - 2 * HALF, W), F32)], axis=0))
    mout_ref[...] = m_rows_t[0:C, 0:bands]
    for cp in out_copies():
        cp.wait()


def solution(mesh):
    nr, nc = mesh.shape["rows"], mesh.shape["cols"]
    rch = ROWS // nc

    def on_device(observed, nonlin, abundance, spectra, kernels, tile_family):
        bands = observed.shape[0]
        vm = pltpu.VMEM
        dma = pltpu.SemaphoreType.DMA
        scratch = [
            vm((PAIRS, 2 * HALF, 2 * W), F32), vm((PAIRS, C, 2 * W), F32), vm((PAIRS, 8, 2 * W), F32),
            vm((4, EXT, C, 2 * W), F32), vm((4, 3, C, W), F32),
            vm((EXT, C, 2 * W), F32), vm((3, C, W), F32), vm((EXT, C, 6 * W), BF),
            vm((4, 4, C, 2 * W), F32), vm((4, 4, C, 2 * W), F32), vm((4, 2, C, W), F32),
            vm((4, 2, 3, C, W), F32), vm((4, 2, C, W), F32), vm((3, C, W), F32),
            vm((5, 6 * W, 2 * W), BF), vm((5, 6 * W, 2 * W), BF),
            vm((3, 3 * W, W), BF), vm((2, 3 * W, W), BF),
            vm((PAIRS, C, 2 * W), F32), vm((PAIRS, 2 * C, 2 * W), BF),
            vm((PAIRS, 2 * HALF, 2 * W), BF), vm((PAIRS, 2 * HALF, 2 * W), BF),
            vm((PAIRS, C, 2 * W), F32), vm((PAIRS, C, 6 * W), BF),
            vm((2 * HALF, W), F32), vm((2 * HALF, 2 * W), BF), vm((W, 2 * HALF), BF), vm((W, 2 * W), BF),
            vm((W, 4 * W), F32),
            vm((ITERS, ROWS, W), F32), vm((ITERS, nc, rch, W), F32), vm((ITERS, rch, W), F32),
            vm((ITERS, nr, rch, W), F32), vm((ITERS + 1, ROWS, W), F32),
            dma((3, H)), dma((4, 8)), dma((4, 8)),
            dma((ITERS,)), dma((ITERS,)), dma((ITERS,)), dma((ITERS,)), dma((ITERS,)), dma((ITERS,)),
        ]
        any_spec = pl.BlockSpec(memory_space=pl.ANY)
        vspec = pl.BlockSpec(memory_space=pltpu.VMEM)
        sspec = pl.BlockSpec(memory_space=pltpu.SMEM)
        out, m_out = pl.pallas_call(
            functools.partial(kernel, nr, nc, bands),
            out_shape=(
                jax.ShapeDtypeStruct(abundance.shape, F32),
                jax.ShapeDtypeStruct((C, bands), F32),
            ),
            in_specs=[any_spec, vspec, any_spec, vspec, sspec, sspec],
            out_specs=(any_spec, vspec),
            scratch_shapes=scratch,
            compiler_params=pltpu.CompilerParams(collective_id=0, has_side_effects=True),
            name="unmix",
        )(observed, nonlin, abundance, spectra.T, jnp.transpose(kernels, (1, 0, 2)), tile_family)
        return out, m_out.T

    placed = (
        P(None, "rows", "cols"), P("rows", "cols"), P(None, "rows", "cols"),
        P(), P(), P("rows", "cols"),
    )
    return jax.shard_map(
        on_device, mesh=mesh, in_specs=placed,
        out_specs=(P(None, "rows", "cols"), P()), check_vma=False,
    )
```

time: 105 us -> 79.1 us (0.75)
  Pallas kernels: 96.5 us -> 74.1 us
  local copies, waits for them, and re-layouts: 6.98 us -> 3.44 us
    pallas_call x1, Pallas kernels: 96.5 us -> 74.1 us  [on_device(): pl.pallas_call(functools.partial(kernel, nr, nc, bands), out_shape=(jax.S...]
    unnamed x4 -> x2, local copies, waits for them, and re-layouts: 6.98 us -> 3.44 us
where the time goes in v2:
time: 79.1 us; the launch traced here: 78.8 us
  Pallas kernels  74.1 us (94%)
  local copies, waits for them, and re-layouts  3.44 us (4%)
  between operations  1.29 us (2%)
    pallas_call x1, Pallas kernels, on_device(): pl.pallas_call(functools.partial(kernel, nr, nc, bands), out_shape=(jax.S...  74.1 us
    unnamed x2, local copies, waits for them, and re-layouts  3.44 us

profile of v2, /device:TPU:1, one launch (start us, length us, event | category | flops | bytes accessed | tf_op | source)
XLA Modules:
  0.0 78.8 jit_solution(17856550133568791146)
XLA Ops:
  1.3 74.1 %unmix.1 = (f32[64,16,128]{2,1,0:T(8,128)}, f32[64,426]{1,0:T(8,128)}) custom-call(f32[426,16,128]{2,1,0:T(8,128)} %obs_hbm.1, f32[16,128]{1,0:T(8,128)} %bend_ref.1, f32[64,16,128]{2,1,0:T(8,128)} %a_hbm.1, f32[64,426]{1,0:T(8,128)} %bitcast.3, f32[9,8,9]{2,1,0:T(8,128)} %bitcast.5, s32[1,1]{1,0:T(1,128)S(6)} %copy.10.fam_ref), custom_call_target="tpu_custom_call" | custom-call | tf_op jit(solution)/shard_map/unmix/pallas_call | solution.py:615
  75.4 1.9 %copy.11 = f32[64,16,128]{2,1,0:T(8,128)} copy(f32[64,16,128]{2,1,0:T(8,128)} %get-tuple-element.8) | data formatting | bytes 1048576
  77.3 1.6 %copy.12 = f32[426,64]{0,1:T(8,128)} copy(f32[426,64]{0,1:T(8,128)} %bitcast.4) | data formatting | bytes 218112

commit v3 on v2

--- a/solution.py
+++ b/solution.py
@@ -10,13 +10,15 @@
 MESH = pl.DeviceIdType.MESH
 KS = 9
 ITERS = 3
+VM_LIMIT = 40 * 1024 * 1024
 BF = jnp.bfloat16
 F32 = jnp.float32
 H, W, C = 16, 128, 64
 PAIRS = H // 2
 EXT = PAIRS + 4
-HALF = 216
-ROWS = 256
+HALF = 224
+BANDS = 432
+REST = BANDS - HALF
 
 
 def split(x):
@@ -36,22 +38,30 @@
     return lax.broadcasted_iota(jnp.int32, shape, dim)
 
 
+def chunks(nc):
+    rch = (HALF // nc + 7) // 8 * 8
+    return rch, HALF // rch
+
+
 def kernel(
     nr, nc, bands,
     obs_hbm, bend_ref, a_hbm, m_ref, kern_ref, fam_ref,
-    out_hbm, mout_ref,
+    a_out, m_out,
     obs_v, a_stage, bend_v, s_main, s_strip, a_main, a_strip, a3,
-    r_up, r_dn, r_one, r_side, v_buf, x_buf,
+    r_up, r_dn, r_one, r_side, r_dg, v_buf, x_buf,
     w3, wt3, fe3, as3,
-    acc_b, bb, wgt_hi, wgt_lo, g_v, g3, gacc, m_lhs, mt_lhs, q_sel, m_t,
+    acc_b, bb, wgt, g_v, g3, gacc, m_lhs, mt_lhs, q_sel, m_t,
     gp, rs_buf, b_src, b_buf, mp,
-    in_sem, ex_s, ex_r, rs_s, rs_r, b_s, b_r, c_s, c_r,
+    in_sem, ex_s, ex_r, dg_s, dg_r, rs_s, rs_r, b_s, b_r, c_s, c_r,
 ):
     r = lax.axis_index("rows")
     c = lax.axis_index("cols")
     has_up, has_dn = r > 0, r < nr - 1
     has_l, has_r = c > 0, c < nc - 1
-    rch = ROWS // nc
+    rch, nown = chunks(nc)
+    grp = nc // 2
+    span = grp * rch
+    owner = c < nown
     npix = float(nr * nc * H * W)
 
     barrier = pltpu.get_barrier_semaphore()
@@ -66,6 +76,15 @@
     @pl.loop(1, nr)
     def _(j):
         greet(lax.rem(r + j, nr), c)
+
+    corners = (
+        (has_up & has_l, -1, -1), (has_up & has_r, -1, 1),
+        (has_dn & has_l, 1, -1), (has_dn & has_r, 1, 1),
+    )
+    for cond, dr, dc in corners:
+        @pl.when(cond)
+        def _(dr=dr, dc=dc):
+            greet(r + dr, c + dc)
 
     a_cp = [
         pltpu.make_async_copy(
@@ -117,10 +136,24 @@
              cp(7, s_main.at[it, pl.ds(2, 2)], r_dn.at[it, pl.ds(2, 2)], up, c)),
         )
         ends = (
-            (has_dn, has_up, cp(2, v_buf.at[it, 1], r_one.at[it, 0], dn, c)),
-            (has_up, has_dn, cp(3, v_buf.at[it, 0], r_one.at[it, 1], up, c)),
+            (has_dn & over, has_up & over, cp(2, v_buf.at[it, 1], r_one.at[it, 0], dn, c)),
+            (has_up & over, has_dn & over, cp(3, v_buf.at[it, 0], r_one.at[it, 1], up, c)),
         )
         return side, rows_a, rows_b, ends
+
+    def corner(k, t, dr, dc):
+        return pltpu.make_async_remote_copy(
+            src_ref=s_strip.at[0, t], dst_ref=r_dg.at[k], send_sem=dg_s.at[k], recv_sem=dg_r.at[k],
+            device_id=(lax.clamp(0, r + dr, nr - 1), lax.clamp(0, c + dc, nc - 1)),
+            device_id_type=MESH,
+        )
+
+    dg = (
+        (corners[3][0], corners[0][0], corner(0, 2, 1, 1)),
+        (corners[2][0], corners[1][0], corner(1, 2, 1, -1)),
+        (corners[1][0], corners[2][0], corner(2, 0, -1, 1)),
+        (corners[0][0], corners[3][0], corner(3, 0, -1, -1)),
+    )
 
     def start(copies):
         for send, _, cp in copies:
@@ -165,6 +198,11 @@
     @pl.when(has_dn)
     def _():
         r_dn[0, 0:2] = jnp.zeros((2, C, 2 * W), F32)
+
+    for k, (cond, _, _) in enumerate(corners):
+        @pl.when(jnp.logical_not(cond))
+        def _(k=k):
+            r_dg[k] = jnp.zeros((C, W), F32)
 
     lane = iota((C, W), 1)
     edge_lane = (lane < 4) | (lane >= W - 4)
@@ -237,9 +275,11 @@
         v = strip_x(col_i & 15) - x_in + 4
         as3[t] = table(index(u, v, u == u))
 
-    pl.semaphore_wait(barrier, nc - 1 + nr - 1)
-    for part in ex(0)[:3]:
-        start(part)
+    pl.semaphore_wait(barrier, nc - 1 + nr - 1 + sum(k[0].astype(jnp.int32) for k in corners))
+    start(dg)
+    first_side, _, first_rows, _ = ex(0)
+    start(first_side)
+    start(first_rows)
 
 
     qr, qc = iota((W, 2 * W), 0), iota((W, 2 * W), 1)
@@ -248,101 +288,128 @@
     m_t[0:C, 0:bands] = m_ref[...]
     m_rows = jnp.transpose(m_t[...])
     gacc[0:full] = m_rows[0:full]
-    gacc[full:] = jnp.zeros((2 * HALF - full, W), F32)
-    gacc[2 * HALF - tail:] = m_rows[full:bands]
+    gacc[full:] = jnp.zeros((BANDS - full, W), F32)
+    gacc[BANDS - tail:] = m_rows[full:bands]
     low = iota((HALF, W), 1) < C
-    rows_2 = iota((HALF, W), 0) + HALF
-    twice = (rows_2 >= full) & (rows_2 < 2 * HALF - tail)
     md0 = gacc[...] + pltpu.roll(gacc[...], C, 1)
-    mp[0, 0:HALF] = jnp.where(low, md0[0:HALF], md0[HALF:])
-    mp[0, HALF:ROWS] = jnp.zeros((ROWS - HALF, W), F32)
-    gp[:, HALF:ROWS] = jnp.zeros((ITERS, ROWS - HALF, W), F32)
+    blank = jnp.zeros((HALF - REST, W), F32)
+    mp[0] = jnp.where(low, md0[0:HALF], jnp.concatenate([md0[HALF:], blank], axis=0))
+    wgt[BANDS:] = jnp.zeros((HALF + 2 * span - BANDS, 2 * PAIRS * 2 * W), BF)
     for h in range(H):
         bend_v[h // 2, :, (h % 2) * W:(h % 2 + 1) * W] = jnp.broadcast_to(
             bend_ref[h:h + 1, :], (8, W)
         )
 
     def spectra_of(k):
-        x = mp[k, 0:HALF]
+        x = mp[k]
         y = pltpu.roll(x, C, 1)
-        return jnp.where(low, x, y), jnp.where(low, y, x)
+        return jnp.concatenate([jnp.where(low, x, y), jnp.where(low, y, x)[0:REST]], axis=0)
 
     def set_spectra(k):
-        a, b = spectra_of(k)
-        hi, lo = split(jnp.concatenate([a, b], axis=0) * (1.0 / C))
+        hi, lo = split(spectra_of(k) * (1.0 / C))
         m_lhs[:, 0:W] = hi
         m_lhs[:, W:] = lo
+
+    def set_transposed():
         mt_lhs[...] = mm_nt(q_sel[...], m_lhs[...]).astype(BF)
 
-    set_spectra(0)
     for cp in o_cp:
         cp.wait()
 
-    def rs_sum_copies(g):
-        whole = rs_buf.at[g, pl.ds(0, nc - 1)]
+    def many(ref, n, g, s_sem, r_sem, dr, dc):
+        whole = ref.at[g, pl.ds(0, n)]
         return pltpu.make_async_remote_copy(
-            src_ref=whole, dst_ref=whole, send_sem=rs_s.at[g], recv_sem=rs_r.at[g],
-            device_id=(r, lax.rem(c + 1, nc)), device_id_type=MESH,
-        )
-
-    def b_sum_copies(g):
-        whole = b_buf.at[g, pl.ds(0, nr - 1)]
-        return pltpu.make_async_remote_copy(
-            src_ref=whole, dst_ref=whole, send_sem=b_s.at[g], recv_sem=b_r.at[g],
-            device_id=(lax.rem(r + 1, nr), c), device_id_type=MESH,
-        )
-
-    def c_sum_copies(g):
-        whole = mp.at[g + 1, pl.ds(0, ROWS - rch)]
+            src_ref=whole, dst_ref=whole, send_sem=s_sem.at[g], recv_sem=r_sem.at[g],
+            device_id=(dr, dc), device_id_type=MESH,
+        )
+
+    next_c, next_r = lax.rem(c + 1, nc), lax.rem(r + 1, nr)
+
+    def rs_many(n, g):
+        return many(rs_buf, n, g, rs_s, rs_r, r, next_c)
+
+    def b_many(g):
+        return many(b_buf, nr - 1, g, b_s, b_r, next_r, c)
+
+    def c_many(rows, g):
+        whole = mp.at[g + 1, pl.ds(0, rows)]
         return pltpu.make_async_remote_copy(
             src_ref=whole, dst_ref=whole, send_sem=c_s.at[g], recv_sem=c_r.at[g],
-            device_id=(r, lax.rem(c + 1, nc)), device_id_type=MESH,
-        )
-
-    mine = pl.ds(pl.multiple_of(c * rch, rch), rch)
-
-    def rs_start(g):
-        rs_buf[g, c] = gp[g, mine]
-
-        @pl.loop(1, nc)
+            device_id=(r, next_c), device_id_type=MESH,
+        )
+
+    def chunk(k):
+        return pl.ds(pl.multiple_of(k * rch, rch), rch)
+
+    def rs_start(g, half):
+        @pl.loop(0, grp)
         def _(j):
-            t = lax.rem(c + j, nc)
-            pltpu.make_async_remote_copy(
-                src_ref=gp.at[g, pl.ds(pl.multiple_of(t * rch, rch), rch)],
-                dst_ref=rs_buf.at[g, c], send_sem=rs_s.at[g], recv_sem=rs_r.at[g],
-                device_id=(r, t), device_id_type=MESH,
-            ).start()
+            k = half * grp + j
+
+            @pl.when((k < nown) & (k != c))
+            def _():
+                pltpu.make_async_remote_copy(
+                    src_ref=gp.at[g, chunk(k)], dst_ref=rs_buf.at[g, c],
+                    send_sem=rs_s.at[g], recv_sem=rs_r.at[g],
+                    device_id=(r, k), device_id_type=MESH,
+                ).start()
 
     def b_start(g):
-        rs_sum_copies(g).wait_recv()
-        total = rs_buf[g, 0]
-        for j in range(1, nc):
-            total = total + rs_buf[g, j]
-        b_src[g] = total
-        b_buf[g, r] = total
-
-        @pl.loop(1, nr)
-        def _(j):
-            pltpu.make_async_remote_copy(
-                src_ref=b_src.at[g], dst_ref=b_buf.at[g, r],
-                send_sem=b_s.at[g], recv_sem=b_r.at[g],
-                device_id=(lax.rem(r + j, nr), c), device_id_type=MESH,
-            ).start()
+        @pl.when(owner)
+        def _():
+            rs_buf[g, c] = gp[g, chunk(c)]
+            rs_many(nc - 1, g).wait_recv()
+            total = rs_buf[g, 0]
+            for j in range(1, nc):
+                total = total + rs_buf[g, j]
+            b_src[g] = total
+            b_buf[g, r] = total
+
+            @pl.loop(1, nr)
+            def _(j):
+                pltpu.make_async_remote_copy(
+                    src_ref=b_src.at[g], dst_ref=b_buf.at[g, r],
+                    send_sem=b_s.at[g], recv_sem=b_r.at[g],
+                    device_id=(lax.rem(r + j, nr), c), device_id_type=MESH,
+                ).start()
 
     def c_start(g):
-        b_sum_copies(g).wait_recv()
-        total = b_buf[g, 0]
-        for j in range(1, nr):
-            total = total + b_buf[g, j]
-        mp[g + 1, mine] = jnp.maximum(mp[g, mine] - 40.0 * (total / npix), 0.0)
-
-        @pl.loop(1, nc)
-        def _(j):
-            pltpu.make_async_remote_copy(
-                src_ref=mp.at[g + 1, mine], dst_ref=mp.at[g + 1, mine],
-                send_sem=c_s.at[g], recv_sem=c_r.at[g],
-                device_id=(r, lax.rem(c + j, nc)), device_id_type=MESH,
-            ).start()
+        @pl.when(owner)
+        def _():
+            b_many(g).wait_recv()
+            total = b_buf[g, 0]
+            for j in range(1, nr):
+                total = total + b_buf[g, j]
+            mine = chunk(c)
+            mp[g + 1, mine] = jnp.maximum(mp[g, mine] - 40.0 * (total / npix), 0.0)
+
+            @pl.loop(1, nc)
+            def _(j):
+                pltpu.make_async_remote_copy(
+                    src_ref=mp.at[g + 1, mine], dst_ref=mp.at[g + 1, mine],
+                    send_sem=c_s.at[g], recv_sem=c_r.at[g],
+                    device_id=(r, lax.rem(c + j, nc)), device_id_type=MESH,
+                ).start()
+
+    def c_wait(g):
+        @pl.when(owner)
+        def _():
+            c_many((nown - 1) * rch, g).wait_recv()
+
+        @pl.when(jnp.logical_not(owner))
+        def _():
+            c_many(nown * rch, g).wait_recv()
+
+    def sent(g):
+        @pl.when(owner)
+        def _():
+            rs_many(nown - 1, g).wait_send()
+            b_many(g).wait_send()
+            many(rs_buf, nc - 1, g, c_s, c_r, r, next_c).wait_send()
+
+        @pl.when(jnp.logical_not(owner))
+        def _():
+            rs_many(nown, g).wait_send()
 
     lane_m = lane & 15
     lane_q = lane >> 4
@@ -423,33 +490,40 @@
                 moved = pltpu.roll(edge, (-8 * h - 4) % W, 1)
                 val = acc_b[p, :, j * W:(j + 1) * W] + jnp.where(edge_lane, moved, 0.0)
                 hi, lo = split(val)
-                bb[p, 0:C, j * W:(j + 1) * W] = hi
-                bb[p, C:, j * W:(j + 1) * W] = lo
-
-    def spectral(it):
-        gacc[...] = jnp.zeros_like(gacc)
-
-        @pl.loop(0, PAIRS, unroll=PAIRS)
-        def _(p):
-            both = bb[p]
+                bb[0:C, h * W:(h + 1) * W] = hi
+                bb[C:, h * W:(h + 1) * W] = lo
+
+    def pair(p, k=0):
+        lo = (k * PAIRS + p) * 2 * W
+        return slice(lo, lo + 2 * W)
+
+    def spectral():
+        for p in range(PAIRS):
+            both = bb[:, pair(p)]
             lin = mm(m_lhs[...], jnp.concatenate([both, both], axis=0))
             t = lin * bend_v[p, 0:1, :]
             a = 1.0 + t
             resid = lin * a - obs_v[p]
             hi, lo = split(resid * (a + t))
-            wgt_hi[p] = hi
-            wgt_lo[p] = lo
-            gacc[...] += mm_nt(hi, both) + mm_nt(lo, both)
-
-        g = gacc[...]
-        g = (g + pltpu.roll(g, C, 1)) * (1.0 / C)
-        second = jnp.where(twice, 0.0, g[HALF:])
-        gp[it, 0:HALF] = jnp.where(low, g[0:HALF], second)
+            wgt[0:BANDS, pair(p)] = hi
+            wgt[0:BANDS, pair(p, 1)] = lo
+
+    low_span = iota((span, W), 1) < C
+    span_row = iota((span, W), 0)
+
+    def spectra_grad(it, half):
+        parts = []
+        for first in (0, HALF):
+            rows = pl.ds(pl.multiple_of(first + half * span, 16), span)
+            g = mm_nt(wgt[rows, 0:PAIRS * 2 * W], bb[...]) + mm_nt(wgt[rows, PAIRS * 2 * W:], bb[...])
+            parts.append((g + pltpu.roll(g, C, 1)) * (1.0 / C))
+        row = span_row + (half * span + HALF)
+        second = jnp.where((row >= full) & (row < BANDS - tail), 0.0, parts[1])
+        gp[it, pl.ds(pl.multiple_of(half * span, 8), span)] = jnp.where(low_span, parts[0], second)
 
     def pixel_grad():
-        @pl.loop(0, PAIRS, unroll=PAIRS)
-        def _(p):
-            part = mm(mt_lhs[...], wgt_hi[p]) + mm(mt_lhs[...], wgt_lo[p])
+        for p in range(PAIRS):
+            part = mm(mt_lhs[...], wgt[0:BANDS, pair(p)]) + mm(mt_lhs[...], wgt[0:BANDS, pair(p, 1)])
             g = part[0:C] + part[C:]
             g_v[p] = g
             g3[p] = lhs3(g)
@@ -491,13 +565,7 @@
             else:
                 s_main[it, 4:8] += res
 
-    def out_copies():
-        return [
-            pltpu.make_async_copy(
-                a_main.at[h // 2 + 2, :, pl.ds((h % 2) * W, W)], out_hbm.at[:, h, :], in_sem.at[0, h]
-            )
-            for h in range(H)
-        ]
+    mine_half = c // grp
 
     @pl.loop(0, ITERS + 1)
     def _(it):
@@ -526,9 +594,18 @@
         def _():
             c_start(it - 1)
 
+        @pl.when(it == 0)
+        def _():
+            wait_recv(dg)
+            for k in range(2):
+                left, right = r_dg[2 * k], r_dg[2 * k + 1]
+                r_one[0, k] = jnp.where(
+                    lane_m >= 8, pltpu.roll(left, 8, 1), pltpu.roll(right, W - 8, 1)
+                )
+
+        wait_recv(ends)
         wait_recv(rows_a)
         wait_recv(rows_b)
-        wait_recv(ends)
         update(it, 0)
         update(it, 2)
 
@@ -536,23 +613,23 @@
         def _():
             blur_outer()
 
-        @pl.when(it == ITERS)
-        def _():
-            for cp in out_copies():
-                cp.start()
+        @pl.when(jnp.logical_not(more))
+        def _():
+            a_out[...] = a_main[2:EXT - 2]
 
         @pl.when(it > 0)
         def _():
-            c_sum_copies(it - 1).wait_recv()
-
-        @pl.when((it > 0) & more)
+            c_wait(it - 1)
+
+        @pl.when(more)
         def _():
             set_spectra(it)
-
-        @pl.when(more)
-        def _():
-            spectral(it)
-            rs_start(it)
+            spectral()
+            spectra_grad(it, 1 - mine_half)
+            rs_start(it, 1 - mine_half)
+            spectra_grad(it, mine_half)
+            rs_start(it, mine_half)
+            set_transposed()
             pixel_grad()
             adjoint_strips(it + 1)
             next_side, next_rows, _, _ = ex(it + 1)
@@ -568,62 +645,89 @@
 
         @pl.when(it > 0)
         def _():
-            rs_sum_copies(it - 1).wait_send()
-            b_sum_copies(it - 1).wait_send()
-            c_sum_copies(it - 1).wait_send()
-
-    a, b = spectra_of(ITERS)
-    gacc[0:HALF] = a
-    gacc[HALF:] = b
-    last = gacc[2 * HALF - tail:]
-    gacc[full:bands] = last
-    m_rows_t = jnp.transpose(jnp.concatenate([gacc[...], jnp.zeros((4 * W - 2 * HALF, W), F32)], axis=0))
-    mout_ref[...] = m_rows_t[0:C, 0:bands]
-    for cp in out_copies():
+            sent(it - 1)
+
+    wait_send(dg)
+    m_out[...] = mp[ITERS]
+
+
+def finish(bands, a_ref, m_ref, a_hbm, mt_ref, m_v, sem):
+    copies = [
+        pltpu.make_async_copy(
+            a_ref.at[h // 2, :, pl.ds((h % 2) * W, W)], a_hbm.at[:, h, :], sem.at[h]
+        )
+        for h in range(H)
+    ]
+    for cp in copies:
+        cp.start()
+    full = bands // 8 * 8
+    tail = bands - full
+    m_v[...] = jnp.zeros_like(m_v)
+    m_v[0:HALF] = m_ref[...]
+    m_v[HALF:BANDS] = pltpu.roll(m_ref[0:REST], C, 1)
+    last = m_v[BANDS - tail:BANDS]
+    m_v[full:bands] = last
+    mt_ref[...] = jnp.transpose(m_v[...])[0:C, 0:bands]
+    for cp in copies:
         cp.wait()
 
 
 def solution(mesh):
     nr, nc = mesh.shape["rows"], mesh.shape["cols"]
-    rch = ROWS // nc
+    rch, _ = chunks(nc)
 
     def on_device(observed, nonlin, abundance, spectra, kernels, tile_family):
         bands = observed.shape[0]
         vm = pltpu.VMEM
         dma = pltpu.SemaphoreType.DMA
         scratch = [
-            vm((PAIRS, 2 * HALF, 2 * W), F32), vm((PAIRS, C, 2 * W), F32), vm((PAIRS, 8, 2 * W), F32),
+            vm((PAIRS, BANDS, 2 * W), F32), vm((PAIRS, C, 2 * W), F32), vm((PAIRS, 8, 2 * W), F32),
             vm((4, EXT, C, 2 * W), F32), vm((4, 3, C, W), F32),
             vm((EXT, C, 2 * W), F32), vm((3, C, W), F32), vm((EXT, C, 6 * W), BF),
             vm((4, 4, C, 2 * W), F32), vm((4, 4, C, 2 * W), F32), vm((4, 2, C, W), F32),
-            vm((4, 2, 3, C, W), F32), vm((4, 2, C, W), F32), vm((3, C, W), F32),
+            vm((4, 2, 3, C, W), F32), vm((4, C, W), F32), vm((4, 2, C, W), F32), vm((3, C, W), F32),
             vm((5, 6 * W, 2 * W), BF), vm((5, 6 * W, 2 * W), BF),
             vm((3, 3 * W, W), BF), vm((2, 3 * W, W), BF),
-            vm((PAIRS, C, 2 * W), F32), vm((PAIRS, 2 * C, 2 * W), BF),
-            vm((PAIRS, 2 * HALF, 2 * W), BF), vm((PAIRS, 2 * HALF, 2 * W), BF),
+            vm((PAIRS, C, 2 * W), F32), vm((2 * C, PAIRS * 2 * W), BF),
+            vm((HALF + nc // 2 * rch * 2, 2 * PAIRS * 2 * W), BF),
             vm((PAIRS, C, 2 * W), F32), vm((PAIRS, C, 6 * W), BF),
-            vm((2 * HALF, W), F32), vm((2 * HALF, 2 * W), BF), vm((W, 2 * HALF), BF), vm((W, 2 * W), BF),
+            vm((BANDS, W), F32), vm((BANDS, 2 * W), BF), vm((W, BANDS), BF), vm((W, 2 * W), BF),
             vm((W, 4 * W), F32),
-            vm((ITERS, ROWS, W), F32), vm((ITERS, nc, rch, W), F32), vm((ITERS, rch, W), F32),
-            vm((ITERS, nr, rch, W), F32), vm((ITERS + 1, ROWS, W), F32),
-            dma((3, H)), dma((4, 8)), dma((4, 8)),
+            vm((ITERS, nc // 2 * rch * 2, W), F32), vm((ITERS, nc, rch, W), F32), vm((ITERS, rch, W), F32),
+            vm((ITERS, nr, rch, W), F32), vm((ITERS + 1, HALF, W), F32),
+            dma((3, H)), dma((4, 8)), dma((4, 8)), dma((4,)), dma((4,)),
             dma((ITERS,)), dma((ITERS,)), dma((ITERS,)), dma((ITERS,)), dma((ITERS,)), dma((ITERS,)),
         ]
-        any_spec = pl.BlockSpec(memory_space=pl.ANY)
+        def held(x):
+            return pltpu.with_memory_space_constraint(x, pltpu.HBM)
+
+        any_spec = pl.BlockSpec(memory_space=pltpu.HBM)
         vspec = pl.BlockSpec(memory_space=pltpu.VMEM)
         sspec = pl.BlockSpec(memory_space=pltpu.SMEM)
         out, m_out = pl.pallas_call(
             functools.partial(kernel, nr, nc, bands),
             out_shape=(
+                jax.ShapeDtypeStruct((PAIRS, C, 2 * W), F32),
+                jax.ShapeDtypeStruct((HALF, W), F32),
+            ),
+            in_specs=[any_spec, vspec, any_spec, vspec, sspec, sspec],
+            out_specs=(vspec, vspec),
+            scratch_shapes=scratch,
+            compiler_params=pltpu.CompilerParams(collective_id=0, has_side_effects=True, vmem_limit_bytes=VM_LIMIT),
+            name="unmix",
+        )(held(observed), held(nonlin), held(abundance), held(spectra.T), held(jnp.transpose(kernels, (1, 0, 2))), tile_family)
+        out, m_out = pl.pallas_call(
+            functools.partial(finish, bands),
+            out_shape=(
                 jax.ShapeDtypeStruct(abundance.shape, F32),
                 jax.ShapeDtypeStruct((C, bands), F32),
             ),
-            in_specs=[any_spec, vspec, any_spec, vspec, sspec, sspec],
-            out_specs=(any_spec, vspec),
-            scratch_shapes=scratch,
-            compiler_params=pltpu.CompilerParams(collective_id=0, has_side_effects=True),
-            name="unmix",
-        )(observed, nonlin, abundance, spectra.T, jnp.transpose(kernels, (1, 0, 2)), tile_family)
+            in_specs=[vspec, vspec],
+            out_specs=(pl.BlockSpec(memory_space=pltpu.HBM), vspec),
+            scratch_shapes=[vm((4 * W, W), F32), dma((H,))],
+            compiler_params=pltpu.CompilerParams(vmem_limit_bytes=8 * 1024 * 1024),
+            name="finish",
+        )(out, m_out)
         return out, m_out.T
 
     placed = (

time: 79.1 us -> 75.7 us (0.957)
  local copies, waits for them, and re-layouts: 3.44 us -> 0 us
    unnamed x2 -> x0, local copies, waits for them, and re-layouts: 3.44 us -> none
    pallas_call x0 -> x1, Pallas kernels: none -> 1.57 us  [on_device(): pl.pallas_call(functools.partial(finish, bands), out_shape=(jax.ShapeDtyp...]
    pallas_call x1, Pallas kernels: 74.1 us -> 72.7 us  [on_device(): pl.pallas_call(functools.partial(kernel, nr, nc, bands), out_shape=(jax.S...]
where the time goes in v3:
time: 75.7 us; the launch traced here: 75.5 us
  Pallas kernels  74.3 us (98%)
  between operations  1.29 us (2%)
    pallas_call x1, Pallas kernels, on_device(): pl.pallas_call(functools.partial(kernel, nr, nc, bands), out_shape=(jax.S...  72.7 us
    pallas_call x1, Pallas kernels, on_device(): pl.pallas_call(functools.partial(finish, bands), out_shape=(jax.ShapeDtyp...  1.57 us

profile of v3, /device:TPU:1, one launch (start us, length us, event | category | flops | bytes accessed | tf_op | source)
XLA Modules:
  0.0 75.5 jit_solution(3817881765428445436)
XLA Ops:
  1.3 72.7 %unmix.1 = (f32[8,64,256]{2,1,0:T(8,128)S(1)}, f32[224,128]{1,0:T(8,128)S(1)}) custom-call(f32[426,16,128]{2,1,0:T(8,128)} %obs_hbm.1, f32[16,128]{1,0:T(8,128)} %bend_ref.1, f32[64,16,128]{2,1,0:T(8,128)} %a_hbm.1, f32[64,426]{1,0:T(8,128)} %bitcast.3, f32[9,8,9]{2,1,0:T(8,128)} %bitcast.4, s32[1,1]{1,0:T(1,128)S(6)} %copy.8.fam_ref), custom_call_target="tpu_custom_call" | custom-call | tf_op jit(solution)/shard_map/unmix/pallas_call | solution.py:707
  74.0 1.6 %finish.1 = (f32[64,16,128]{2,1,0:T(8,128)}, f32[64,426]{1,0:T(8,128)}) custom-call(f32[8,64,256]{2,1,0:T(8,128)S(1)} %get-tuple-element.6.a_ref, f32[224,128]{1,0:T(8,128)S(1)} %get-tuple-element.7.m_ref), custom_call_target="tpu_custom_call" | custom-call | tf_op jit(solution)/shard_map/finish/pallas_call | solution.py:719

commit v4 on v3

--- a/solution.py
+++ b/solution.py
@@ -512,11 +512,17 @@
     span_row = iota((span, W), 0)
 
     def spectra_grad(it, half):
-        parts = []
-        for first in (0, HALF):
-            rows = pl.ds(pl.multiple_of(first + half * span, 16), span)
-            g = mm_nt(wgt[rows, 0:PAIRS * 2 * W], bb[...]) + mm_nt(wgt[rows, PAIRS * 2 * W:], bb[...])
-            parts.append((g + pltpu.roll(g, C, 1)) * (1.0 / C))
+        first, second = (
+            pl.ds(pl.multiple_of(k * HALF + half * span, 16), span) for k in range(2)
+        )
+        n = PAIRS * 2 * W
+        lhs = jnp.concatenate(
+            [wgt[first, 0:n], wgt[second, 0:n], wgt[first, n:], wgt[second, n:]], axis=0
+        )
+        g = mm_nt(lhs, bb[...])
+        g = g[0:2 * span] + g[2 * span:]
+        g = (g + pltpu.roll(g, C, 1)) * (1.0 / C)
+        parts = (g[0:span], g[span:])
         row = span_row + (half * span + HALF)
         second = jnp.where((row >= full) & (row < BANDS - tail), 0.0, parts[1])
         gp[it, pl.ds(pl.multiple_of(half * span, 8), span)] = jnp.where(low_span, parts[0], second)

time: 75.7 us -> 78.5 us (1.037)
  Pallas kernels: 74.3 us -> 77.1 us
    pallas_call x1, Pallas kernels: 72.7 us -> 75.5 us  [on_device(): pl.pallas_call(functools.partial(kernel, nr, nc, bands), out_shape=(jax.S...]
where the time goes in v4:
time: 78.5 us; the launch traced here: 78.4 us
  Pallas kernels  77.1 us (98%)
  between operations  1.29 us (2%)
    pallas_call x1, Pallas kernels, on_device(): pl.pallas_call(functools.partial(kernel, nr, nc, bands), out_shape=(jax.S...  75.5 us
    pallas_call x1, Pallas kernels, on_device(): pl.pallas_call(functools.partial(finish, bands), out_shape=(jax.ShapeDtyp...  1.57 us

profile of v4, /device:TPU:1, one launch (start us, length us, event | category | flops | bytes accessed | tf_op | source)
XLA Modules:
  0.0 78.4 jit_solution(8427943896398356183)
XLA Ops:
  1.3 75.5 %unmix.1 = (f32[8,64,256]{2,1,0:T(8,128)S(1)}, f32[224,128]{1,0:T(8,128)S(1)}) custom-call(f32[426,16,128]{2,1,0:T(8,128)} %obs_hbm.1, f32[16,128]{1,0:T(8,128)} %bend_ref.1, f32[64,16,128]{2,1,0:T(8,128)} %a_hbm.1, f32[64,426]{1,0:T(8,128)} %bitcast.3, f32[9,8,9]{2,1,0:T(8,128)} %bitcast.4, s32[1,1]{1,0:T(1,128)S(6)} %copy.8.fam_ref), custom_call_target="tpu_custom_call" | custom-call | tf_op jit(solution)/shard_map/unmix/pallas_call | solution.py:713
  76.8 1.6 %finish.1 = (f32[64,16,128]{2,1,0:T(8,128)}, f32[64,426]{1,0:T(8,128)}) custom-call(f32[8,64,256]{2,1,0:T(8,128)S(1)} %get-tuple-element.6.a_ref, f32[224,128]{1,0:T(8,128)S(1)} %get-tuple-element.7.m_ref), custom_call_target="tpu_custom_call" | custom-call | tf_op jit(solution)/shard_map/finish/pallas_call | solution.py:725
